TPU v7x, 32 devices: a whole 2x2x4 slice. The times are simulated.
32 devices in a mesh: gx: 4 (over y, core), gy: 8 (over z, x).
Axes of the slice: x: 2, y: 2, z: 4, core: 2. Of those that a mesh axis runs over, the one named last changes fastest.
Arguments:
- source: float32 [128, 128, 128], P('gx', 'gy'), may hold values from -30 to 30
- permittivity: float32 [128, 128, 128], P('gx', 'gy'), may hold values from 2 to 80
- screening: float32 [128, 128, 128], P('gx', 'gy'), may hold values from 0 to 16
- potential: float32 [128, 128, 128], P('gx', 'gy'), may hold values from -3 to 3
- fixed_cell: int32 [128, 128, 128], P('gx', 'gy'), may hold values 0 or 1
Outputs:
- result: float32 [128, 128, 128], P('gx', 'gy')
All inputs are finite; a program needn't handle non-finite values. No bound on the sum of `fixed_cell` on one device may be relied on, other than what follows from the above.
Results may differ from a plain program's by a relative error of at most 0.0003.
Values sent between devices are 32-bit elements; how exact they have to be, the bound alone decides.
No kernel may reach another device: no remote copies, remote signals or barrier semaphores. Data moves between devices by JAX's collectives and lax.ppermute only.
A program may use at most 128 MiB of HBM per device.

v0:
```python
import jax
import jax.numpy as jnp
from jax import lax
from jax.experimental import pallas as pl
from jax.experimental.pallas import tpu as pltpu
from jax.sharding import PartitionSpec as P

F32 = jnp.float32
BX, BY, NL = 32, 16, 128
YE = 24
X1 = BX // 2
H1 = 8
G1 = X1 + 2 * H1
NF = X1 + 4
NM = G1 // 2 + 2
STATE = 16
GF = 3
GM = 8
LN2 = 0.6931471805599453


def rot(value, shift, axis):
    return pltpu.roll(value, shift % value.shape[axis], axis)


def iota(shape, axis):
    return lax.broadcasted_iota(jnp.int32, shape, axis)


def sds(*shape):
    return jax.ShapeDtypeStruct(shape, F32)


def by_parity(axis, action):
    odd = lax.axis_index(axis) % 2

    @pl.when(odd == 0)
    def _():
        action(0, 1)

    @pl.when(odd == 1)
    def _():
        action(1, 0)


def call(kernel, out_shape, scratch=(), vmem=24, hbm=0, alias=None):
    specs = {"in_specs": [pl.BlockSpec(memory_space=pltpu.HBM)] * hbm} if hbm else {}
    return pl.pallas_call(
        kernel,
        out_shape=out_shape,
        **specs,
        input_output_aliases=alias or {},
        scratch_shapes=list(scratch),
        compiler_params=pltpu.CompilerParams(vmem_limit_bytes=vmem << 20),
    )


YROWS = 10 * BX
XROWS = 12 * 8
FIELDS = (3, 3, 2, 2, 2)


def split_rows(ref, at):
    one, two = ref[pl.ds(at, 4, stride=2), :], ref[pl.ds(at + 1, 4, stride=2), :]
    lane = iota((4, NL), 1)
    even = (lane % 4 + lane // 4) % 2 == 0
    return jnp.concatenate([jnp.where(even, one, two), jnp.where(even, two, one)], axis=0)


def pack_y(hpot, hper, hsrc, hscr, hfix, pot, per, src, scr, fix, p2, out0, out1, xm0, xm1, sems, t, pk):
    outs, mains = (out0, out1), (xm0, xm1)
    pairs = ((hpot, pot), (hper, per), (hsrc, src), (hscr, scr), (hfix, fix))
    copies = [pltpu.make_async_copy(a, b, sems.at[k]) for k, (a, b) in enumerate(pairs)]
    for k in (1, 0, 2, 3, 4):
        copies[k].start()
    copies[1].wait()
    zlane = iota((BX // 2, NL), 1)

    def free_of(value):
        return jnp.where(value == 0, F32(1.0), F32(0.0))

    def row(ref, r):
        return ref[pl.ds(r, BX, stride=BY), :]

    def half(ref, r, parity):
        even = ref[pl.ds(r, BX // 2, stride=2 * BY), :]
        odd = ref[pl.ds(BY + r, BX // 2, stride=2 * BY), :]
        return jnp.where((r + zlane) % 2 == parity, even, odd)

    def side(out, r1, r2, r3):
        rows = [
            row(pot, r1), row(per, r1), row(src, r1), row(scr, r1), free_of(row(fix, r1)),
            row(pot, r2), row(per, r2), free_of(row(fix, r2)),
        ]
        for k, value in enumerate(rows):
            out[BX * k : BX * (k + 1), :] = value
        base = BX * len(rows)
        for k, value in enumerate([half(pot, r3, 1), half(per, r3, 1), half(src, r2, 0), half(scr, r2, 0)]):
            out[base + k * BX // 2 : base + (k + 1) * BX // 2, :] = value

    v = per[...].reshape(BX // 4, 4, BY, NL)
    v = (v[:, 0] + v[:, 1]) + (v[:, 2] + v[:, 3])
    t[...] = lane_pairs(lane_pairs(v, 1), 2).reshape(BX // 4 * BY, NL)
    n2 = BX // 4
    lane = iota((n2, NL), 1)
    total = None
    for j in range(4):
        r = [t[pl.ds(4 * j + k, n2, stride=BY), :] for k in range(4)]
        value = (r[0] + r[1]) + (r[2] + r[3])
        total = value if total is None else jnp.where(lane % 4 == j, value, total)
    pk[...] = F32(1.0 / 64) * total
    p2[...] = split_rows(pk, 0)
    for k in (0, 2, 3, 4):
        copies[k].wait()

    def action(hi, lo):
        side(outs[hi], BY - 1, BY - 2, BY - 3)
        side(outs[lo], 0, 1, 2)
        for out in outs:
            out[YROWS : YROWS + 8, :] = p2[...]

    by_parity("gy", action)

    def slab(out, planes):
        k = 0
        for ref, depth in zip((pot, per, src, scr, fix), FIELDS, strict=True):
            for x in planes[:depth]:
                value = ref[BY * x : BY * (x + 1), :]
                out[BY * k : BY * (k + 1), :] = free_of(value) if ref is fix else value
                k += 1

    def action_x(hi, lo):
        slab(mains[hi], (BX - 1, BX - 2, BX - 3))
        slab(mains[lo], (0, 1, 2))

    by_parity("gx", action_x)


def pack_x(p2, got0, got1, hpot, hper, hsrc, hscr, hfree, out0, out1):
    gots, outs = (got0, got1), (out0, out1)
    halos = (hpot, hper, hsrc, hscr, hfree)
    for h in halos:
        h[...] = jnp.zeros_like(h)

    def place(got, slots):
        def whole(ref, k, slot):
            ref[pl.ds(slot, BX, stride=8), :] = got[BX * k : BX * (k + 1), :]

        def halved(ref, k, slot):
            value = got[BX * 8 + k * BX // 2 : BX * 8 + (k + 1) * BX // 2, :]
            ref[pl.ds(slot, BX // 2, stride=16), :] = value
            ref[pl.ds(8 + slot, BX // 2, stride=16), :] = value

        s1, s2, s3 = slots
        for k, ref in enumerate(halos):
            whole(ref, k, s1)
        whole(hpot, 5, s2)
        whole(hper, 6, s2)
        whole(hfree, 7, s2)
        halved(hpot, 0, s3)
        halved(hper, 1, s3)
        halved(hsrc, 2, s2)
        halved(hscr, 3, s2)

    def action_y(hi, lo):
        place(gots[hi], (0, 1, 2))
        place(gots[lo], (7, 6, 5))

    by_parity("gy", action_y)

    def slab(out, planes):
        k = 0
        for h, depth in zip(halos, FIELDS, strict=True):
            for x in planes[:depth]:
                out[8 * k : 8 * (k + 1), :] = h[8 * x : 8 * (x + 1), :]
                k += 1

    def action_p(hi, lo):
        for out in outs:
            out[XROWS : XROWS + 8, :] = p2[...]
            out[XROWS + 8 : XROWS + 16, :] = gots[hi][YROWS : YROWS + 8, :]
            out[XROWS + 16 : XROWS + 24, :] = gots[lo][YROWS : YROWS + 8, :]

    by_parity("gy", action_p)

    def action_x(hi, lo):
        slab(outs[hi], (BX - 1, BX - 2, BX - 3))
        slab(outs[lo], (0, 1, 2))

    by_parity("gx", action_x)


def nonlinear(u, scr):
    up = jnp.exp(u - F32(LN2))
    down = jnp.exp(-u - F32(LN2))
    return scr * (up - down), scr * (up + down)


def colour_mask(n, zstep):
    shape = (n, YE, NL)
    return (iota(shape, 1) + iota(shape, 2) // zstep) % 2 == 0


def beside_of(other, colour, faces, at, n, zstep):
    fin, fout, fyp, fym, fzp, fzm = faces
    here = pl.ds(at, n)
    v = other[1 - colour, pl.ds(at - 1, n + 2)]
    mid = v[1 : n + 1]
    first = colour_mask(n, zstep)
    across = jnp.where(first, v[:n], v[2:]) if colour == 0 else jnp.where(first, v[2:], v[:n])
    return (
        (fin[here] * mid + fout[colour, here] * across)
        + (fyp[colour, here] * rot(mid, -1, 1) + fym[colour, here] * rot(mid, 1, 1))
        + (fzp[colour, here] * rot(mid, -zstep, 2) + fzm[colour, here] * rot(mid, zstep, 2))
    )


def pairs_of(u, at, n, colour, refs):
    c, fin, fout, fyp, fym, fzp, fzm, src, scr, _ = refs
    here = pl.ds(at, n)
    plane = u[colour, here]
    sh, ch = nonlinear(plane, scr[colour, here])
    centre = c[colour, here]
    beside = beside_of(u, colour, (fin, fout, fyp, fym, fzp, fzm), at, n, 1)
    return plane, centre * plane - beside + sh - src[colour, here], centre, ch


def fine_new(u, at, n, colour, refs):
    plane, value, centre, ch = pairs_of(u, at, n, colour, refs)
    return jnp.where(refs[-1][colour, pl.ds(at, n)] > 0.5, plane - value / (centre + ch), plane)


def fine_half(u, at, n, colour, refs):
    u[colour, pl.ds(at, n)] = fine_new(u, at, n, colour, refs)


def groups(first, count, n, step):
    assert count % n == 0

    def one(g, _):
        step(first + g * n)
        return 0

    lax.fori_loop(0, count // n, one, 0, unroll=True)


def faces_of(p, at, n, scale, zstep, fin, fout, fyp, fym, fzp, fzm):
    here = pl.ds(at, n)
    lane = iota((n, YE, NL), 2)
    first = colour_mask(n, zstep)
    half = F32(0.5 * scale)
    for colour in (0, 1):
        plane = p[colour, here]
        v = p[1 - colour, pl.ds(at - 1, n + 2)]
        mid = v[1 : n + 1]
        across = jnp.where(first, v[:n], v[2:]) if colour == 0 else jnp.where(first, v[2:], v[:n])
        if colour == 0:
            fin[here] = half * (plane + mid)
        fout[colour, here] = half * (plane + across)
        fyp[colour, here] = half * (plane + rot(mid, -1, 1))
        fym[colour, here] = half * (plane + rot(mid, 1, 1))
        fzp[colour, here] = jnp.where(lane >= NL - zstep, F32(0.0), half * (plane + rot(mid, -zstep, 2)))
        fzm[colour, here] = jnp.where(lane < zstep, F32(0.0), half * (plane + rot(mid, zstep, 2)))


def lane_pairs(value, step):
    lane = iota(value.shape, value.ndim - 1)
    return value + jnp.where((lane // step) % 2 == 0, rot(value, -step, value.ndim - 1), rot(value, step, value.ndim - 1))


def fine_begin(state, at, n):
    u, ep, c, fin, fout, fyp, fym, fzp, fzm, esrc, escr, efree = state[:12]
    faces_of(ep, at, n, 1.0, 1, fin, fout, fyp, fym, fzp, fzm)
    here = pl.ds(at, n)
    lane = iota((n, YE, NL), 2)
    for colour in (0, 1):
        ends = jnp.where((lane == 0) | (lane == NL - 1), F32(0.5) * ep[colour, here], F32(0.0))
        c[colour, here] = (
            (fin[here] + fout[colour, here]) + (fyp[colour, here] + fym[colour, here])
            + (fzp[colour, here] + fzm[colour, here]) + ends
        )
    fine_half(u, at, n, 0, (c, fin, fout, fyp, fym, fzp, fzm, esrc, escr, efree))


def fine_own(pot, per, src, scr, fix, hpot, hper, hsrc, hscr, hfree, *state):
    u, ep, c, fin, fout, fyp, fym, fzp, fzm, esrc, escr, efree = state[:12]
    first = colour_mask(1, 1)[0]

    def own(k, _):
        for ref, h, ext in ((pot, hpot, u), (per, hper, ep), (src, hsrc, esrc), (scr, hscr, escr), (fix, hfree, efree)):
            value = ref[pl.ds(pl.multiple_of(2 * k * BY, 8), 2 * BY), :]
            if ref is fix:
                value = jnp.where(value == 0, F32(1.0), F32(0.0))
            halo = h[pl.ds(pl.multiple_of(16 * k, 8), 16), :]
            for rows, one, two in (
                (slice(0, BY), value[:BY], value[BY:]),
                (slice(BY, YE), halo[:8], halo[8:]),
            ):
                ext[0, k + 2, rows, :] = jnp.where(first[rows], one, two)
                ext[1, k + 2, rows, :] = jnp.where(first[rows], two, one)
        return 0

    lax.fori_loop(0, X1, own, 0, unroll=4)
    groups(3, X1 - 2, 2, lambda at: fine_begin(state, at, 2))
    refs = (c, fin, fout, fyp, fym, fzp, fzm, esrc, escr, efree)
    groups(4, X1 - 4, 3, lambda at: fine_half(u, at, 3, 1, refs))
    groups(6, X1 - 8, 4, lambda at: fine_down(state, at, 4))
    for k in range(1, X1 + 1):
        fine_coarse_p(state, k)


def fine_down(state, at, n):
    u, _, c, fin, fout, fyp, fym, fzp, fzm, esrc, escr, efree, tr, tc = state[:14]
    refs = (c, fin, fout, fyp, fym, fzp, fzm, esrc, escr, efree)
    left, react = F32(0.0), F32(0.0)
    for colour in (0, 1):
        _, value, _, ch = pairs_of(u, at, n, colour, refs)
        left += jnp.where(efree[colour, pl.ds(at, n)] > 0.5, -value, F32(0.0))
        react += ch
    to = pl.multiple_of((at - 2) * BY, 8)
    tr[pl.ds(to, n * BY), :] = lane_pairs(left[:, 0:BY], 1).reshape(n * BY, NL)
    tc[pl.ds(to, n * BY), :] = lane_pairs(react[:, 0:BY], 1).reshape(n * BY, NL)


def fine_coarse_p(state, k):
    ep, tp, p1 = state[1], state[14], state[15]
    at = k * YE
    tp[at : at + YE, :] = lane_pairs(ep[0, k + 1] + ep[1, k + 1], 1)
    p1[k] = F32(0.125) * (tp[pl.ds(at, 8, stride=2), :] + tp[pl.ds(at + 1, 8, stride=2), :])


def fine_pre(goty0, goty1, xm0, xm1, got0, got1, *refs_):
    state, refs_ = refs_[STATE : 2 * STATE], refs_[2 * STATE :]
    u, ep, c, fin, fout, fyp, fym, fzp, fzm, esrc, escr, efree, tr, tc, tp, p1 = state
    csum, g1, m0, m1, n0, n1 = refs_
    gots, mains, outs, nexts = (got0, got1), (xm0, xm1), (m0, m1), (n0, n1)
    first = colour_mask(1, 1)[0]

    def place(main, got, near, far, flip):
        k = 0
        for ext, depth in zip((u, ep, esrc, escr, efree), FIELDS, strict=True):
            planes = []
            for _ in range(depth):
                rows = main[BY * k : BY * (k + 1), :]
                planes.append(jnp.concatenate([rows, got[8 * k : 8 * (k + 1), :]], axis=0))
                k += 1
            one, two = (planes[1], planes[0]) if flip else (planes[0], planes[1])
            ext[0, near] = jnp.where(first, one, two)
            ext[1, near] = jnp.where(first, two, one)
            third = planes[2] if depth == 3 else jnp.zeros((YE, NL), F32)
            ext[0, far] = third
            ext[1, far] = third

    def action_x(hi, lo):
        place(mains[hi], gots[hi], X1 + 2, X1 + 3, False)
        place(mains[lo], gots[lo], 1, 0, True)

    by_parity("gx", action_x)
    refs = (c, fin, fout, fyp, fym, fzp, fzm, esrc, escr, efree)

    for at in (1, X1 + 1):
        fine_begin(state, at, 2)
    for at in (1, X1):
        fine_half(u, at, 3, 1, refs)
    for at in (2, X1 - 2):
        fine_down(state, at, 4)
    for k in (0, X1 + 1):
        fine_coarse_p(state, k)

    eighth = F32(0.125)
    sub = iota((8, NL), 0)
    lane = iota((8, NL), 1)

    first8 = (sub + lane // 2) % 2 == 0

    def coarse(x1):
        k = x1 + 1
        p = p1[k]
        base = k * YE
        high = eighth * (tp[pl.ds(base + 2, 8, stride=2), :] + tp[pl.ds(base + 3, 8, stride=2), :])
        edge = tp[pl.ds(pl.multiple_of(base + 16, 8), 8), :]
        edge = eighth * (edge + rot(edge, 1, 0))
        low = jnp.where(sub == 0, rot(edge, 1, 0), rot(p, 1, 0))
        front = jnp.where(lane >= NL - 2, F32(0.0), rot(p, -2, 1))
        back = jnp.where(lane < 2, F32(0.0), rot(p, 2, 1))
        near = (p1[k + 1] + p1[k - 1]) + (high + low) + (front + back)
        centre = F32(3.0) * p + F32(0.5) * near
        at = x1 * BY
        r = eighth * (tr[pl.ds(at, 8, stride=2), :] + tr[pl.ds(at + 1, 8, stride=2), :])
        react = eighth * (tc[pl.ds(at, 8, stride=2), :] + tc[pl.ds(at + 1, 8, stride=2), :])
        diag = F32(0.25) * centre + react
        message = jnp.where(lane % 2 == 0, r, F32(1.0) / diag)
        m0[pl.ds(pl.multiple_of(x1 * 8, 8), 8), :] = message
        m1[pl.ds(pl.multiple_of(x1 * 8, 8), 8), :] = message
        return diag, react

    def make(k, _):
        diag0, react0 = coarse(2 * k)
        diag1, react1 = coarse(2 * k + 1)
        csum[k] = react0 + react1
        g1[0, k] = jnp.where(first8, diag0, diag1)
        g1[1, k] = jnp.where(first8, diag1, diag0)
        return 0

    lax.fori_loop(0, X1 // 2, make, 0, unroll=4)

    for a in range(X1 // 2):
        message = jnp.where(lane % 2 == 0, p1[1 + 2 * a], p1[2 + 2 * a])
        for m in outs:
            m[X1 * 8 + 8 * a : X1 * 8 + 8 * a + 8, :] = message

    base = X1 * 8 + X1 * 4

    def odd_row(out, y):
        out[base : base + X1, :] = u[1, pl.ds(2, X1), y, :]

    def slab(out, at, x):
        out[0 : H1 * 8, :] = m0[8 * at : 8 * (at + H1), :]
        row = X1 * 8 + 4 * at
        out[H1 * 8 : H1 * 12, :] = m0[row : row + H1 * 4, :]
        out[XOWN:XMAIN, :] = u[1, x, 0:BY, :]

    def action_next(hi, lo):
        slab(nexts[hi], X1 - H1, X1 + 1)
        slab(nexts[lo], 0, 2)

    by_parity("gx", action_next)

    def action_y(hi, lo):
        odd_row(outs[hi], BY - 2)
        odd_row(outs[lo], 1)
        outs[hi][base + X1 : base + X1 + 8, :] = (goty0, goty1)[lo][YROWS : YROWS + 8, :]
        outs[lo][base + X1 : base + X1 + 8, :] = (goty0, goty1)[hi][YROWS : YROWS + 8, :]

    by_parity("gy", action_y)


def halo_rows(dx):
    return (16 * (dx - 1), 2) if dx < 5 else (64 + 8 * (dx - 5), 1)


def halo_pair(t):
    return (96 + 16 * t, 2) if t < 2 else (128 + 8 * (t - 2), 1)


P2AT = 144
YMSG = X1 * 8 + X1 * 4 + BX // 2 + 8
XOWN = H1 * 8 + (H1 // 2) * 8
XMAIN = XOWN + BY
XMSG = P2AT + 40


def pack_x1(got0, got1, fx0, fx1, out0, out1):
    gots, outs, fines = (got0, got1), (out0, out1), (fx0, fx1)
    odd_y = lax.axis_index("gy") % 2
    upper = iota((8, NL), 0) < 4

    def go(hi, lo):
        def put(out, at, count, row):
            above, below = gots[hi][row : row + 8, :], gots[lo][row : row + 8, :]
            if count == 2:
                out[at : at + 8, :] = above
                out[at + 8 : at + 16, :] = below
            else:
                out[at : at + 8, :] = jnp.where(upper, above, below)

        def slab(out, near, step, behind):
            for dx in range(1, H1 + 1):
                put(out, *halo_rows(dx), 8 * (near + step * (dx - 1)))
            for t in range(H1 // 2):
                put(out, *halo_pair(t), X1 * 8 + 8 * (near // 2 + step * t))
            out[P2AT : P2AT + 8, :] = gots[hi][YMSG - 8 : YMSG, :]
            out[P2AT + 8 : P2AT + 16, :] = gots[lo][YMSG - 8 : YMSG, :]
            out[P2AT + 16 : P2AT + 40, :] = behind[XROWS : XROWS + 24, :]

        def action(xhi, xlo):
            slab(outs[xhi], X1 - 1, -1, fines[xlo])
            slab(outs[xlo], 0, 1, fines[xhi])

        by_parity("gx", action)

    @pl.when(odd_y == 0)
    def _():
        go(0, 1)

    @pl.when(odd_y == 1)
    def _():
        go(1, 0)


def coarse_half(e, r, d, at, n, colour, faces, zstep):
    here = pl.ds(at, n)
    e[colour, here] = (r[colour, here] + beside_of(e, colour, faces, at, n, zstep)) * d[colour, here]


def dup_even(value):
    lane = iota(value.shape, value.ndim - 1)
    return jnp.where(lane % 2 == 0, value, rot(value, 1, value.ndim - 1))


def dup_odd(value):
    lane = iota(value.shape, value.ndim - 1)
    return jnp.where(lane % 2 == 1, value, rot(value, -1, value.ndim - 1))


MIDS = 10


def mid_put(state, k, rows, one, two, both):
    _, r, d, p = state[:4]
    mask = colour_mask(1, 2)[0][rows]
    for colour in (0, 1):
        a, b = (one, two) if colour == 0 else (two, one)
        value = jnp.where(mask, a, b)
        r[colour, k, rows, :] = dup_even(value)
        d[colour, k, rows, :] = dup_odd(value)
    a, b = dup_even(both), dup_odd(both)
    p[0, k, rows, :] = jnp.where(mask, a, b)
    p[1, k, rows, :] = jnp.where(mask, b, a)


def mid_begin(state, at, n):
    e, r, d, p, *faces = state
    here = pl.ds(at, n)
    faces_of(p, at, n, 0.25, 2, *faces)
    e[0, here] = r[0, here] * d[0, here]


def mid_own(m0, gy0, gy1, *state):
    gys = (gy0, gy1)
    e, r, d, p, *faces = state

    def own(hi, lo):
        for k in range(X1 // 2):
            for j, ref in enumerate((m0, gys[hi], gys[lo])):
                two = ref[16 * k : 16 * k + 16, :]
                both = ref[X1 * 8 + 8 * k : X1 * 8 + 8 * k + 8, :]
                mid_put(state, 1 + H1 // 2 + k, slice(8 * j, 8 * j + 8), two[:8], two[8:], both)

    by_parity("gy", own)
    first = 2 + H1 // 2
    groups(first, X1 // 2 - 2, 2, lambda at: mid_begin(state, at, 2))
    groups(first + 1, X1 // 2 - 4, 2, lambda at: coarse_half(e, r, d, at, 2, 1, faces, 2))


def mid_pre(xm0, xm1, gx0, gx1, csum, g1, *refs_):
    gxs, mains = (gx0, gx1), (xm0, xm1)
    state, refs_ = refs_[MIDS : 2 * MIDS], refs_[2 * MIDS :]
    e, r, d, p, *faces = state
    fin, fout, fyp, fym, fzp, fzm = faces
    msg, t, tr, tc, pc, pk = refs_

    def beyond(main, ref, at, far):
        def whole(row, start, count):
            own_rows = main[row : row + 8, :]
            above = ref[start : start + 8, :]
            below = ref[start + 8 : start + 16, :] if count == 2 else above
            return jnp.concatenate([own_rows, above, below], axis=0)

        for k in range(H1 // 2):
            one, two = (whole(8 * a, *halo_rows(H1 - a if far else a + 1)) for a in (2 * k, 2 * k + 1))
            both = whole(H1 * 8 + 8 * k, *halo_pair(H1 // 2 - 1 - k if far else k))
            mid_put(state, at + k, slice(0, YE), one, two, both)

    def action(hi, lo):
        beyond(mains[hi], gxs[hi], 1 + H1 // 2 + X1 // 2, False)
        beyond(mains[lo], gxs[lo], 1, True)

    by_parity("gx", action)
    for ref in (p, e):
        for colour in (0, 1):
            ref[colour, 0] = jnp.zeros((YE, NL), F32)
            ref[colour, NM - 1] = jnp.zeros((YE, NL), F32)
    inner = 1 + H1 // 2
    for at in (*range(1, inner + 1), *range(inner + X1 // 2 - 1, NM - 1)):
        mid_begin(state, at, 1)
    for at in (1, inner + X1 // 2 - 2):
        coarse_half(e, r, d, at, inner + 1, 1, faces, 2)
    for colour in (0, 1):
        groups(1, NM - 2, GM, lambda at, colour=colour: coarse_half(e, r, d, at, GM, colour, faces, 2))

    def down(at):
        n = 4
        here = pl.ds(at, n)
        k = pl.ds(at - 1 - H1 // 2, n)
        left = F32(0.0)
        for colour in (0, 1):
            part = r[colour, here] + beside_of(e, colour, faces, at, n, 2)
            left += part[:, 0:8] - g1[colour, k] * e[colour, here, 0:8, :]
        to = pl.multiple_of((at - 1 - H1 // 2) * 8, 8)
        tr[pl.ds(to, n * 8), :] = lane_pairs(left, 2).reshape(n * 8, NL)
        tc[pl.ds(to, n * 8), :] = lane_pairs(csum[k], 2).reshape(n * 8, NL)

    groups(1 + H1 // 2, X1 // 2, 4, down)

    def coarse_p(x2, _):
        t[pl.ds(pl.multiple_of(x2 * YE, 8), YE), :] = lane_pairs(p[0, x2 + 1] + p[1, x2 + 1], 2)
        return 0

    lax.fori_loop(0, G1 // 2, coarse_p, 0, unroll=4)

    eighth = F32(0.125)
    n2, m2 = X1 // 2, G1 // 2

    def compact(ref, first, rows, stride):
        lane = iota((rows, NL), 1)
        out = None
        for j in range(4):
            value = ref[pl.ds(first + 2 * j, rows, stride=stride), :] + ref[pl.ds(first + 2 * j + 1, rows, stride=stride), :]
            out = value if out is None else jnp.where(lane % 4 == j, value, out)
        return eighth * out

    r2 = compact(tr, 0, n2, 8)
    react2 = compact(tc, 0, n2, 8)
    for k in range(3):
        pc[k] = compact(t, 8 * k, m2, YE)
    h2 = H1 // 2
    centre_p = pc[0, h2 : h2 + n2, :]
    j4 = iota((n2, NL), 1) % 4
    lane = iota((n2, NL), 1)
    high = jnp.where(j4 < 3, rot(centre_p, -1, 1), rot(pc[1, h2 : h2 + n2, :], 3, 1))
    low = jnp.where(j4 > 0, rot(centre_p, 1, 1), rot(pc[2, h2 : h2 + n2, :], -3, 1))
    front = jnp.where(lane >= NL - 4, F32(0.0), rot(centre_p, -4, 1))
    back = jnp.where(lane < 4, F32(0.0), rot(centre_p, 4, 1))
    near = (pc[0, h2 + 1 : h2 + 1 + n2, :] + pc[0, h2 - 1 : h2 - 1 + n2, :]) + (high + low) + (front + back)
    diag2 = F32(0.0625) * (F32(3.0) * centre_p + F32(0.5) * near) + react2
    for k, value in enumerate((r2, F32(1.0) / diag2, centre_p)):
        pk[8 * k : 8 * k + 8, :] = value
    r2, inverse2, own_p = (split_rows(pk, 8 * k) for k in range(3))
    near_rows = iota((8, NL), 1) % 4 >= 2
    ahead = jnp.where(near_rows, r2, rot(own_p, -2, 1))
    behind = jnp.where(near_rows, rot(own_p, 2, 1), r2)
    count = lax.axis_size("gy")
    place = lax.axis_index("gy")

    def every(k, _):
        step = k % count - place
        msg[k, 0:8, :] = jnp.where(step == 3, ahead, jnp.where(step == -3, behind, r2))
        msg[k, 8:16, :] = inverse2
        return 0

    lax.fori_loop(0, msg.shape[0], every, 0, unroll=8)


def finish(at, got, p2own, yf0, yf1, xf0, xf1, e, r, d, fin1, fout1, fyp1, fym1, fzp1, fzm1,
           before, c, fin, fout, fyp, fym, fzp, fzm, src, scr, free, gy0, gy1, xm0, xm1, gx0, gx1,
           result,
           e2, p2, r2, d2, k2, blk, tx, eu, u, hal, res, sems):
    wx, wy = got.shape[0], got.shape[1]
    rows = wx * 4
    ox, oy = at
    blk[...] = jnp.zeros_like(blk)
    for b in (0, wy + 1):
        for colour in (0, 1):
            e2[colour, b] = jnp.zeros((rows, NL), F32)

    def keep(da, db, ref, first):
        blk[oy + db + 3, ox + da + 2] = ref[first : first + 8, :]

    keep(0, 0, p2own, 0)

    def blocks_y(hi, lo):
        for db, k in ((1, hi), (-1, lo)):
            keep(0, db, (yf0, yf1)[k], YROWS)
            keep(0, 2 * db, (gy0, gy1)[k], YMSG - 8)

    by_parity("gy", blocks_y)

    def blocks_x(hi, lo):
        for da, k in ((1, hi), (-1, lo)):
            fine, mid = (xf0, xf1)[k], (gx0, gx1)[k]
            for n, db in enumerate((0, 1, -1)):
                keep(da, db, fine, XROWS + 8 * n)
                keep(2 * da, db, mid, P2AT + 16 + 8 * n)
            keep(da, 2, mid, P2AT)
            keep(da, -2, mid, P2AT + 8)

    by_parity("gx", blocks_x)
    l4 = iota((8, NL), 1) % 4
    for db in (3, -3):

        @pl.when((oy + db >= 0) & (oy + db < wy))
        def _(db=db):
            for a in range(wx):
                value = got[a, oy + db, 0:8, :]
                value = jnp.where(l4 < 2, rot(value, -2, 1), F32(0.0)) if db > 0 else jnp.where(l4 >= 2, rot(value, 2, 1), F32(0.0))
                blk[oy + db + 3, a + 2] = value

    def spread(b, _):
        for a in range(wx):
            for colour in (0, 1):
                own, to = slice(4 * colour, 4 * colour + 4), slice(4 * a, 4 * a + 4)
                r2[colour, b, to, :] = got[a, b, own, :]
                d2[colour, b, to, :] = got[a, b, 8 + 4 * colour : 12 + 4 * colour, :]
                p2[colour, b + 1, to, :] = blk[b + 3, a + 2, own, :]
        return 0

    lax.fori_loop(0, wy, spread, 0, unroll=4)
    for b in (0, wy + 1):
        for colour in (0, 1):
            p2[colour, b] = jnp.zeros((rows, NL), F32)
    shape = (wy, rows, NL)
    sub, lane = iota(shape, 1), iota(shape, 2)
    j4 = lane % 4
    even = (j4 + lane // 4) % 2 == 0

    def around(ref, colour):
        v = ref[1 - colour]
        mid = v[1 : wy + 1]
        one, two = rot(mid, 1, 1), rot(mid, -1, 1)
        return (
            mid,
            jnp.where(even, one, two) if colour == 0 else jnp.where(even, two, one),
            jnp.where(j4 < 3, rot(mid, -1, 2), rot(v[2:], 3, 2)),
            jnp.where(j4 > 0, rot(mid, 1, 2), rot(v[:wy], -3, 2)),
            rot(mid, -4, 2), rot(mid, 4, 2),
        )

    for colour in (0, 1):
        at_first = even if colour == 0 else ~even
        outside = (at_first & (sub == 0)) | (~at_first & (sub == rows - 1))
        edges = (None, outside, None, None, lane >= NL - 4, lane < 4)
        mine = p2[colour, 1 : wy + 1]
        for k, (value, edge) in enumerate(zip(around(p2, colour), edges, strict=True)):
            face = F32(0.03125) * (mine + value)
            k2[colour, k] = face if edge is None else jnp.where(edge, F32(0.0), face)
    e2[0, 1 : wy + 1] = r2[0] * d2[0]

    def half2(colour):
        total = r2[colour]
        for k, value in enumerate(around(e2, colour)):
            total = total + k2[colour, k] * value
        e2[colour, 1 : wy + 1] = total * d2[colour]

    half2(1)

    def sweep2(_, carry):
        half2(0)
        half2(1)
        return carry

    lax.fori_loop(0, 3, sweep2, 0, unroll=True)

    s8, l8 = iota((8, NL), 0), iota((8, NL), 1)
    even8 = (l8 % 4 + l8 // 4) % 2 == 0
    start = 4 * ox - 2
    inside = (s8 + start >= 0) & (s8 + start < rows)
    for k, step in enumerate((0, 1, -1)):
        near = []
        for colour in (0, 1):
            block = pltpu.roll(e2[colour, oy + step + 1], (rows - start) % rows, 0)[0:8]
            near.append(jnp.where(inside, block, F32(0.0)))
        planes = (jnp.where(even8, near[0], near[1]), jnp.where(even8, near[1], near[0]))
        for second in (0, 1):
            for j in range(4):
                value = jnp.where(l8 % 4 == 0, rot(planes[second], -j, 1), F32(0.0))
                value = value + rot(value, 1, 1)
                value = value + rot(value, 2, 1)
                for y in (0, 1):
                    tx[pl.ds(second * YE + 8 * k + 2 * j + y, 8, stride=2 * YE), :] = value

    def correct(x2, _):
        value = tx[pl.ds(pl.multiple_of(x2 * YE, 8), YE), :]
        for colour in (0, 1):
            eu[colour, x2 + 1] = e[colour, x2 + 1] + value
        return 0

    lax.fori_loop(0, G1 // 2, correct, 0, unroll=4)
    faces1 = (fin1, fout1, fyp1, fym1, fzp1, fzm1)
    for at1, count, n, colour in ((3, 12, 4, 0), (3, 12, 4, 1), (4, 10, 5, 0), (4, 10, 5, 1)):
        groups(at1, count, n, lambda at, n=n, colour=colour: coarse_half(eu, r, d, at, n, colour, faces1, 2))

    base = X1 * 8 + X1 * 4

    def action_y(hi, lo):
        hal[pl.ds(1, X1, stride=8), :] = (gy0, gy1)[hi][base : base + X1, :]
        hal[pl.ds(6, X1, stride=8), :] = (gy0, gy1)[lo][base : base + X1, :]

    by_parity("gy", action_y)
    first = colour_mask(1, 1)[0]
    first1 = colour_mask(1, 2)[0]
    added = (s8 == 1) | (s8 == 6)
    own_rows = slice(0, BY)

    def widen(k, plane, now1, halo1):
        for y in (0, 1):
            tx[pl.ds(k * YE + y, 8, stride=2), :] = plane[0:8]
        wide = tx[pl.ds(pl.multiple_of(k * YE, 8), BY), :]
        hi, lo = plane[8:16], plane[16:24]
        halo = jnp.where(s8 < 2, jnp.where(s8 == 0, hi, rot(hi, 1, 0)), jnp.where(s8 == 7, lo, rot(lo, -1, 0)))
        now = ((before[0, k, own_rows, :], before[0, k, BY:YE, :]), (now1, halo1))
        for colour in (0, 1):
            one, two = now[colour]
            u[colour, k, own_rows, :] = jnp.where(free[colour, k, own_rows, :] > 0.5, one + wide, one)
            u[colour, k, BY:YE, :] = jnp.where(free[colour, k, BY:YE, :] > 0.5, two + halo, two)

    def level1_plane(m, second):
        one, two = (eu[1, m], eu[0, m]) if second else (eu[0, m], eu[1, m])
        return jnp.where(first1, one, two)

    def add(m, _):
        for second in (0, 1):
            k = 2 * m + second + 2
            halo = jnp.where(added, hal[pl.ds(pl.multiple_of(8 * (k - 2), 8), 8), :], before[1, k, BY:YE, :])
            widen(k, level1_plane(m + 1 + H1 // 2, second), before[1, k, own_rows, :], halo)
        return 0

    lax.fori_loop(0, X1 // 2, add, 0, unroll=4)

    def action_x(hi, lo):
        row = (xm0, xm1)[hi][XOWN:XMAIN, :]
        k = X1 + 2
        now = jnp.where(first[own_rows], row, before[1, k, own_rows, :])
        widen(k, level1_plane(1 + H1 // 2 + X1 // 2, 0), now, before[1, k, BY:YE, :])
        row = (xm0, xm1)[lo][XOWN:XMAIN, :]
        now = jnp.where(first[own_rows], before[1, 1, own_rows, :], row)
        widen(1, level1_plane(H1 // 2, 1), now, before[1, 1, BY:YE, :])

    by_parity("gx", action_x)
    for k in (0, NF - 1):
        u[1, k] = before[1, k]
    refs = (c, fin, fout, fyp, fym, fzp, fzm, src, scr, free)
    groups(1, X1 + 2, GF, lambda at: fine_half(u, at, GF, 0, refs))

    def last(at):
        n = 4
        new = fine_new(u, at, n, 1, refs)[:, own_rows]
        even = u[0, pl.ds(at, n), own_rows, :]
        mask = first[own_rows]
        for k in range(n):
            to = pl.multiple_of((at - 2 + k) * 2 * BY, 8)
            res[pl.ds(to, BY), :] = jnp.where(mask, even[k], new[k])
            res[pl.ds(to + BY, BY), :] = jnp.where(mask, new[k], even[k])

    copies = []
    for g in range(X1 // 4):
        last(2 + 4 * g)
        part = pl.ds(g * 8 * BY, 8 * BY)
        copies.append(pltpu.make_async_copy(res.at[part], result.at[part], sems.at[g]))
        copies[-1].start()
    for copy in copies:
        copy.wait()


def swap(pair, axis):
    count = lax.axis_size(axis)
    got = [None, None]
    for first in (1, 0):
        route = []
        for i in range(first, count - 1, 2):
            route += [(i, i + 1), (i + 1, i)]
        got[first] = lax.ppermute(pair[first], axis, route)
    return tuple(got)


def body(source, permittivity, screening, potential, fixed_cell):
    gx, gy = lax.axis_size("gx"), lax.axis_size("gy")
    args = [a.reshape(BX * BY, NL) for a in (potential, permittivity, source, screening, fixed_cell)]
    args = [pltpu.with_memory_space_constraint(a, pltpu.HBM) for a in args]

    whole = (sds(BX * BY, NL),) * 4 + (jax.ShapeDtypeStruct((BX * BY, NL), jnp.int32),)
    *args, p2, y0, y1, xm0, xm1 = call(
        pack_y,
        whole + (sds(8, NL),) + (sds(YROWS + 8, NL),) * 2 + (sds(12 * BY, NL),) * 2,
        [pltpu.SemaphoreType.DMA((5,)), pltpu.VMEM((BX // 4 * BY, NL), F32), pltpu.VMEM((8, NL), F32)],
        hbm=5,
    )(*args)
    y0 = (y0, y1)
    y0 = swap(y0, "gy")
    xm = swap((xm0, xm1), "gx")
    *halos, x0, x1 = call(pack_x, (sds(BX * 8, NL),) * 5 + (sds(XROWS + 24, NL),) * 2)(p2, *y0)
    gotx = swap((x0, x1), "gx")

    ext, one = (2, NF, YE, NL), (NF, YE, NL)
    fields = (sds(*ext),) * 3 + (sds(*one),) + (sds(*ext),) * 8
    fields += (sds(X1 * BY, NL),) * 2 + (sds((X1 + 2) * YE, NL), sds(X1 + 2, 8, NL))
    state = call(fine_own, fields)(*args, *halos)
    fine = call(
        fine_pre,
        fields + (sds(X1 // 2, 8, NL), sds(2, X1 // 2, 8, NL)) + (sds(YMSG, NL),) * 2 + (sds(XMAIN, NL),) * 2,
        alias={6 + k: k for k in range(STATE)},
    )(*y0, *xm, *gotx, *state)
    state, (c1, g1, m0, m1, *xm1) = (fine[0], *fine[2:12]), fine[STATE:]
    goty1 = swap((m0, m1), "gy")
    xm1 = swap(xm1, "gx")
    x1msg = call(pack_x1, (sds(XMSG, NL),) * 2)(*goty1, *gotx)
    gotx1 = swap(x1msg, "gx")

    mid, mid1 = (2, NM, YE, NL), (NM, YE, NL)
    fields1 = (sds(*mid),) * 4 + (sds(*mid1),) + (sds(*mid),) * 5
    level1 = call(mid_own, fields1)(m0, *goty1)
    *level1, message = call(
        mid_pre,
        fields1 + (sds(gx * gy, 16, NL),),
        [
            pltpu.VMEM((G1 // 2 * YE, NL), F32),
            pltpu.VMEM((X1 // 2 * 8, NL), F32),
            pltpu.VMEM((X1 // 2 * 8, NL), F32),
            pltpu.VMEM((3, G1 // 2, NL), F32),
            pltpu.VMEM((24, NL), F32),
        ],
        alias={6 + k: k for k in range(MIDS)},
    )(*xm1, *gotx1, c1, g1, *level1)
    level1 = (*level1[:3], *level1[4:])

    gathered = lax.all_to_all(message, ("gx", "gy"), 0, 0).reshape(gx, gy, 16, NL)
    wx, wy = min(gx, 6), min(gy, 8)
    if (wx, wy) != (gx, gy):
        first = (*window(gx, gy, wx, wy)[:2], 0, 0)
        gathered = lax.dynamic_slice(gathered, first, (wx, wy, 16, NL))

    inputs = (gathered, p2, *y0, *gotx, *level1, *state, *goty1, *xm1, *gotx1)
    result = pl.pallas_call(
        finish_kernel(len(inputs), (gx, gy, wx, wy)),
        out_shape=sds(BX * BY, NL),
        scratch_shapes=[
            pltpu.VMEM((2, wy + 2, wx * 4, NL), F32),
            pltpu.VMEM((2, wy + 2, wx * 4, NL), F32),
            pltpu.VMEM((2, wy, wx * 4, NL), F32),
            pltpu.VMEM((2, wy, wx * 4, NL), F32),
            pltpu.VMEM((2, 6, wy, wx * 4, NL), F32),
            pltpu.VMEM((wy + 6, wx + 4, 8, NL), F32),
            pltpu.VMEM((NF * YE, NL), F32),
            pltpu.VMEM(mid, F32),
            pltpu.VMEM(ext, F32),
            pltpu.VMEM((BX // 2 * 8, NL), F32),
            pltpu.VMEM((BX * BY, NL), F32),
            pltpu.SemaphoreType.DMA((X1 // 4,)),
        ],
        out_specs=pl.BlockSpec(memory_space=pltpu.HBM),
        compiler_params=pltpu.CompilerParams(vmem_limit_bytes=24 << 20),
        name="finish",
    )(*inputs)
    return result.reshape(BX, BY, NL)


def window(gx, gy, wx, wy):
    ix, iy = lax.axis_index("gx"), lax.axis_index("gy")
    fx = jnp.clip(ix - 2, 0, gx - wx)
    fy = jnp.clip(iy - 3, 0, gy - wy)
    return fx, fy, ix - fx, iy - fy


def finish_kernel(count, sizes):
    def kernel(*refs):
        ins, result, scratch = list(refs[:count]), refs[count], list(refs[1 + count :])
        finish(window(*sizes)[2:], *ins, result, *scratch)

    return kernel


def solution(mesh):
    placed = (P("gx", "gy", None),) * 5

    return jax.shard_map(body, mesh=mesh, in_specs=placed, out_specs=P("gx", "gy", None), check_vma=False)
```

profile of v0, /device:TPU:1, one launch (start us, length us, event | category | flops | bytes accessed | tf_op | source)
XLA Modules:
  0.0 56.3 jit_solution(17629571943546832046)
XLA Ops:
  0.0 1.5 %shard_map.55 = (f32[512,128]{1,0:T(8,128)S(1)}, f32[512,128]{1,0:T(8,128)S(1)}, f32[512,128]{1,0:T(8,128)S(1)}, f32[512,128]{1,0:T(8,128)S(1)}, s32[512,128]{1,...) custom-call(f32[512,128]{1,0:T(8,128)} %bitcast.8, ...), custom_call_target="tpu_custom_call" | custom-call | tf_op jit(solution)/shard_map/pallas_call | solution.py:862
  1.5 2.1 %collective-permute-start = (f32[328,128]{1,0:T(8,128)S(1)}, f32[328,128]{1,0:T(8,128)S(1)}, u32[]{:S(2)}, u32[]{:S(2)}) collective-permute-start(f32[328,128]{1,0:T(8,128)S(1)} %get-tuple-element.77), channel_id=1, source_target_pairs={{0,1},{1,0},{2,3},{3,2},{4,5},{5,4},{6,7},{7,6},{8,9},{9,8},{10,11... | collective-permute-start | bytes 503816 | tf_op jit(solution)/shard_map/ppermute | solution.py:852
  3.6 0.7 %collective-permute-start.1 = (f32[328,128]{1,0:T(8,128)S(1)}, f32[328,128]{1,0:T(8,128)S(1)}, u32[]{:S(2)}, u32[]{:S(2)}) collective-permute-start(f32[328,128]{1,0:T(8,128)S(1)} %get-tuple-element.78), channel_id=1, source_target_pairs={{1,2},{2,1},{3,4},{4,3},{5,6},{6,5},{9,10},{10,9},{11,12},{12,11},... | collective-permute-start | bytes 503816 | tf_op jit(solution)/shard_map/ppermute | solution.py:852
  4.3 1.0 %collective-permute-start.2 = (f32[192,128]{1,0:T(8,128)S(1)}, f32[192,128]{1,0:T(8,128)S(1)}, u32[]{:S(2)}, u32[]{:S(2)}) collective-permute-start(f32[192,128]{1,0:T(8,128)S(1)} %get-tuple-element.79), channel_id=1, source_target_pairs={{0,8},{8,0},{16,24},{24,16},{1,9},{9,1},{17,25},{25,17},{2,10},{10... | collective-permute-start | bytes 294920 | tf_op jit(solution)/shard_map/ppermute | solution.py:852
  5.3 3.0 %collective-permute-start.3 = (f32[192,128]{1,0:T(8,128)S(1)}, f32[192,128]{1,0:T(8,128)S(1)}, u32[]{:S(2)}, u32[]{:S(2)}) collective-permute-start(f32[192,128]{1,0:T(8,128)S(1)} %get-tuple-element.80), channel_id=1, source_target_pairs={{8,16},{16,8},{9,17},{17,9},{10,18},{18,10},{11,19},{19,11},{12,20... | collective-permute-start | bytes 294920 | tf_op jit(solution)/shard_map/ppermute | solution.py:852
  8.4 0.0 collective-permute-done.got0.goty0.refs_2_
  8.4 0.0 collective-permute-done.1.got1.goty1.refs_3_
  8.4 0.2 shard_map.56
  8.6 3.4 %collective-permute-start.4 = (f32[120,128]{1,0:T(8,128)S(1)}, f32[120,128]{1,0:T(8,128)S(1)}, u32[]{:S(2)}, u32[]{:S(2)}) collective-permute-start(f32[120,128]{1,0:T(8,128)S(1)} %get-tuple-element.82), channel_id=1, source_target_pairs={{0,8},{8,0},{16,24},{24,16},{1,9},{9,1},{17,25},{25,17},{2,10},{10... | collective-permute-start | bytes 184328 | tf_op jit(solution)/shard_map/ppermute | solution.py:852
  12.0 3.0 %collective-permute-start.5 = (f32[120,128]{1,0:T(8,128)S(1)}, f32[120,128]{1,0:T(8,128)S(1)}, u32[]{:S(2)}, u32[]{:S(2)}) collective-permute-start(f32[120,128]{1,0:T(8,128)S(1)} %get-tuple-element.83), channel_id=1, source_target_pairs={{8,16},{16,8},{9,17},{17,9},{10,18},{18,10},{11,19},{19,11},{12,20... | collective-permute-start | bytes 184328 | tf_op jit(solution)/shard_map/ppermute | solution.py:852
  15.1 1.4 %shard_map.57 = (f32[2,20,24,128]{3,2,1,0:T(8,128)S(1)}, f32[2,20,24,128]{3,2,1,0:T(8,128)S(1)}, f32[2,20,24,128]{3,2,1,0:T(8,128)S(1)}, f32[20,24,128]{2,1,0:T(...) custom-call(f32[512,128]{1,0:T(8,128)S(1)} %get-tuple-element.84.pot, ...), custom_call_target="tpu_custom_call" | custom-call | tf_op jit(solution)/shard_map/pallas_call | solution.py:877
  16.5 0.0 collective-permute-done.2.xm0
  16.5 0.0 collective-permute-done.3.xm1
  16.5 0.0 collective-permute-done.4.got0.fx0.refs_4_
  16.5 1.0 %collective-permute-done.5.got1.fx1.refs_5_ = f32[120,128]{1,0:T(8,128)S(1)} collective-permute-done((f32[120,128]{1,0:T(8,128)S(1)}, f32[120,128]{1,0:T(8,128)S(1)}, u32[]{:S(2)}, u32[]{:S(2)}) %collective-permute-start.5) | collective-permute-done | bytes 61472 | tf_op jit(solution)/shard_map/ppermute | solution.py:852
  17.5 0.9 %shard_map.58 = (f32[2,20,24,128]{3,2,1,0:T(8,128)S(1)}, f32[2,20,24,128]{3,2,1,0:T(8,128)S(1)}, f32[2,20,24,128]{3,2,1,0:T(8,128)S(1)}, f32[20,24,128]{2,1,0:T(...) custom-call(f32[328,128]{1,0:T(8,128)S(1)} %collective-permute-done., ...), custom_call_target="tpu_custom_call", output_to_operand_aliasing={{0}: (6, {}), {1}: (7, {}), {2}: (8, {}), {3}: (9, {}), {4}... | custom-call | tf_op jit(solution)/shard_map/pallas_call | solution.py:878
  18.4 0.7 %collective-permute-start.9 = (f32[216,128]{1,0:T(8,128)S(1)}, f32[216,128]{1,0:T(8,128)S(1)}, u32[]{:S(2)}, u32[]{:S(2)}) collective-permute-start(f32[216,128]{1,0:T(8,128)S(1)} %get-tuple-element.113), channel_id=1, source_target_pairs={{1,2},{2,1},{3,4},{4,3},{5,6},{6,5},{9,10},{10,9},{11,12},{12,11},... | collective-permute-start | bytes 331784 | tf_op jit(solution)/shard_map/ppermute | solution.py:852
  19.1 5.1 %collective-permute-start.8 = (f32[216,128]{1,0:T(8,128)S(1)}, f32[216,128]{1,0:T(8,128)S(1)}, u32[]{:S(2)}, u32[]{:S(2)}) collective-permute-start(f32[216,128]{1,0:T(8,128)S(1)} %get-tuple-element.112.m0), channel_id=1, source_target_pairs={{0,1},{1,0},{2,3},{3,2},{4,5},{5,4},{6,7},{7,6},{8,9},{9,8},{10,11... | collective-permute-start | bytes 331784 | tf_op jit(solution)/shard_map/ppermute | solution.py:852
  24.2 0.0 collective-permute-done.9.got1.gy1.refs_27_
  24.2 2.1 %collective-permute-done.8.got0.gy0.refs_26_ = f32[216,128]{1,0:T(8,128)S(1)} collective-permute-done((f32[216,128]{1,0:T(8,128)S(1)}, f32[216,128]{1,0:T(8,128)S(1)}, u32[]{:S(2)}, u32[]{:S(2)}) %collective-permute-start.8) | collective-permute-done | bytes 110624 | tf_op jit(solution)/shard_map/ppermute | solution.py:852
  26.4 0.1 collective-permute-start.10
  26.5 4.2 %collective-permute-start.11 = (f32[184,128]{1,0:T(8,128)S(1)}, f32[184,128]{1,0:T(8,128)S(1)}, u32[]{:S(2)}, u32[]{:S(2)}) collective-permute-start(f32[184,128]{1,0:T(8,128)S(1)} %get-tuple-element.115), channel_id=1, source_target_pairs={{8,16},{16,8},{9,17},{17,9},{10,18},{18,10},{11,19},{19,11},{12,20... | collective-permute-start | bytes 282632 | tf_op jit(solution)/shard_map/ppermute | solution.py:852
  30.7 0.1 collective-permute-start.6
  30.8 1.9 %collective-permute-start.7 = (f32[112,128]{1,0:T(8,128)S(1)}, f32[112,128]{1,0:T(8,128)S(1)}, u32[]{:S(2)}, u32[]{:S(2)}) collective-permute-start(f32[112,128]{1,0:T(8,128)S(1)} %get-tuple-element.111), channel_id=1, source_target_pairs={{8,16},{16,8},{9,17},{17,9},{10,18},{18,10},{11,19},{19,11},{12,20... | collective-permute-start | bytes 172040 | tf_op jit(solution)/shard_map/ppermute | solution.py:852
  32.7 0.4 shard_map.60
  33.1 0.0 collective-permute-done.6.xm0.refs_28_
  33.1 3.1 %collective-permute-done.7.xm1.refs_29_ = f32[112,128]{1,0:T(8,128)S(1)} collective-permute-done((f32[112,128]{1,0:T(8,128)S(1)}, f32[112,128]{1,0:T(8,128)S(1)}, u32[]{:S(2)}, u32[]{:S(2)}) %collective-permute-start.7) | collective-permute-done | bytes 57376 | tf_op jit(solution)/shard_map/ppermute | solution.py:852
  36.3 0.0 collective-permute-done.10.gx0.refs_30_
  36.3 0.0 collective-permute-done.11.gx1.refs_31_
  36.3 1.7 %shard_map.61 = (f32[2,18,24,128]{3,2,1,0:T(8,128)S(1)}, f32[2,18,24,128]{3,2,1,0:T(8,128)S(1)}, f32[2,18,24,128]{3,2,1,0:T(8,128)S(1)}, f32[2,18,24,128]{3,2,1,...) custom-call(f32[112,128]{1,0:T(8,128)S(1)} %collective-permute-done., ...), custom_call_target="tpu_custom_call", output_to_operand_aliasing={{0}: (6, {}), {1}: (7, {}), {2}: (8, {}), {3}: (9, {}), {4}... | custom-call | tf_op jit(solution)/shard_map/pallas_call | solution.py:892
  37.9 14.7 %all_to_all.5 = f32[32,16,128]{2,1,0:T(8,128)S(1)} all-to-all(f32[32,16,128]{2,1,0:T(8,128)S(1)} %get-tuple-element.128), channel_id=1, replica_groups=mesh['gx'=4,'gy'=8] {'gx','gy'}, dimensions={0} | all-to-all | bytes 524288 | tf_op jit(solution)/shard_map/all_to_all | solution.py:906
  52.7 3.6 %finish.1 = f32[512,128]{1,0:T(8,128)} custom-call(f32[4,8,16,128]{3,2,1,0:T(8,128)S(1)} %bitcast.7, f32[8,128]{1,0:T(8,128)S(1)} %get-tuple-element.81.p2.refs_1_, f32[328,128]{1,0:T(8,128)S(1)} %collective-permute-done.got0.goty0.refs_2_, f32[328,128]{1,0:T(8,128)S(1)} %collective-permute-done.1.got1.goty1.refs_3_, ...), custom_call_target="tpu_custom_call" | custom-call | tf_op jit(solution)/shard_map/finish/pallas_call | solution.py:913
  (1 shorter events, 0.0 us)
Async XLA Ops:
  1.5 6.8 %collective-permute-start = (f32[328,128]{1,0:T(8,128)S(1)}, f32[328,128]{1,0:T(8,128)S(1)}, u32[]{:S(2)}, u32[]{:S(2)}) collective-permute-start(f32[328,128]{1,0:T(8,128)S(1)} %get-tuple-element.77), channel_id=1, source_target_pairs={{0,1},{1,0},{2,3},{3,2},{4,5},{5,4},{6,7},{7,6},{8,9},{9,8},{10,11... | collective-permute-start | bytes 503816 | tf_op jit(solution)/shard_map/ppermute | solution.py:852
  3.6 4.8 %collective-permute-start.1 = (f32[328,128]{1,0:T(8,128)S(1)}, f32[328,128]{1,0:T(8,128)S(1)}, u32[]{:S(2)}, u32[]{:S(2)}) collective-permute-start(f32[328,128]{1,0:T(8,128)S(1)} %get-tuple-element.78), channel_id=1, source_target_pairs={{1,2},{2,1},{3,4},{4,3},{5,6},{6,5},{9,10},{10,9},{11,12},{12,11},... | collective-permute-start | bytes 503816 | tf_op jit(solution)/shard_map/ppermute | solution.py:852
  4.3 12.2 %collective-permute-start.2 = (f32[192,128]{1,0:T(8,128)S(1)}, f32[192,128]{1,0:T(8,128)S(1)}, u32[]{:S(2)}, u32[]{:S(2)}) collective-permute-start(f32[192,128]{1,0:T(8,128)S(1)} %get-tuple-element.79), channel_id=1, source_target_pairs={{0,8},{8,0},{16,24},{24,16},{1,9},{9,1},{17,25},{25,17},{2,10},{10... | collective-permute-start | bytes 294920 | tf_op jit(solution)/shard_map/ppermute | solution.py:852
  5.3 11.2 %collective-permute-start.3 = (f32[192,128]{1,0:T(8,128)S(1)}, f32[192,128]{1,0:T(8,128)S(1)}, u32[]{:S(2)}, u32[]{:S(2)}) collective-permute-start(f32[192,128]{1,0:T(8,128)S(1)} %get-tuple-element.80), channel_id=1, source_target_pairs={{8,16},{16,8},{9,17},{17,9},{10,18},{18,10},{11,19},{19,11},{12,20... | collective-permute-start | bytes 294920 | tf_op jit(solution)/shard_map/ppermute | solution.py:852
  8.6 7.9 %collective-permute-start.4 = (f32[120,128]{1,0:T(8,128)S(1)}, f32[120,128]{1,0:T(8,128)S(1)}, u32[]{:S(2)}, u32[]{:S(2)}) collective-permute-start(f32[120,128]{1,0:T(8,128)S(1)} %get-tuple-element.82), channel_id=1, source_target_pairs={{0,8},{8,0},{16,24},{24,16},{1,9},{9,1},{17,25},{25,17},{2,10},{10... | collective-permute-start | bytes 184328 | tf_op jit(solution)/shard_map/ppermute | solution.py:852
  12.0 5.5 %collective-permute-start.5 = (f32[120,128]{1,0:T(8,128)S(1)}, f32[120,128]{1,0:T(8,128)S(1)}, u32[]{:S(2)}, u32[]{:S(2)}) collective-permute-start(f32[120,128]{1,0:T(8,128)S(1)} %get-tuple-element.83), channel_id=1, source_target_pairs={{8,16},{16,8},{9,17},{17,9},{10,18},{18,10},{11,19},{19,11},{12,20... | collective-permute-start | bytes 184328 | tf_op jit(solution)/shard_map/ppermute | solution.py:852
  18.4 5.8 %collective-permute-start.9 = (f32[216,128]{1,0:T(8,128)S(1)}, f32[216,128]{1,0:T(8,128)S(1)}, u32[]{:S(2)}, u32[]{:S(2)}) collective-permute-start(f32[216,128]{1,0:T(8,128)S(1)} %get-tuple-element.113), channel_id=1, source_target_pairs={{1,2},{2,1},{3,4},{4,3},{5,6},{6,5},{9,10},{10,9},{11,12},{12,11},... | collective-permute-start | bytes 331784 | tf_op jit(solution)/shard_map/ppermute | solution.py:852
  19.1 7.3 %collective-permute-start.8 = (f32[216,128]{1,0:T(8,128)S(1)}, f32[216,128]{1,0:T(8,128)S(1)}, u32[]{:S(2)}, u32[]{:S(2)}) collective-permute-start(f32[216,128]{1,0:T(8,128)S(1)} %get-tuple-element.112.m0), channel_id=1, source_target_pairs={{0,1},{1,0},{2,3},{3,2},{4,5},{5,4},{6,7},{7,6},{8,9},{9,8},{10,11... | collective-permute-start | bytes 331784 | tf_op jit(solution)/shard_map/ppermute | solution.py:852
  26.4 9.9 %collective-permute-start.10 = (f32[184,128]{1,0:T(8,128)S(1)}, f32[184,128]{1,0:T(8,128)S(1)}, u32[]{:S(2)}, u32[]{:S(2)}) collective-permute-start(f32[184,128]{1,0:T(8,128)S(1)} %get-tuple-element.114), channel_id=1, source_target_pairs={{0,8},{8,0},{16,24},{24,16},{1,9},{9,1},{17,25},{25,17},{2,10},{10... | collective-permute-start | bytes 282632 | tf_op jit(solution)/shard_map/ppermute | solution.py:852
  26.5 9.8 %collective-permute-start.11 = (f32[184,128]{1,0:T(8,128)S(1)}, f32[184,128]{1,0:T(8,128)S(1)}, u32[]{:S(2)}, u32[]{:S(2)}) collective-permute-start(f32[184,128]{1,0:T(8,128)S(1)} %get-tuple-element.115), channel_id=1, source_target_pairs={{8,16},{16,8},{9,17},{17,9},{10,18},{18,10},{11,19},{19,11},{12,20... | collective-permute-start | bytes 282632 | tf_op jit(solution)/shard_map/ppermute | solution.py:852
  30.7 2.5 %collective-permute-start.6 = (f32[112,128]{1,0:T(8,128)S(1)}, f32[112,128]{1,0:T(8,128)S(1)}, u32[]{:S(2)}, u32[]{:S(2)}) collective-permute-start(f32[112,128]{1,0:T(8,128)S(1)} %get-tuple-element.110), channel_id=1, source_target_pairs={{0,8},{8,0},{16,24},{24,16},{1,9},{9,1},{17,25},{25,17},{2,10},{10... | collective-permute-start | bytes 172040 | tf_op jit(solution)/shard_map/ppermute | solution.py:852
  30.8 5.5 %collective-permute-start.7 = (f32[112,128]{1,0:T(8,128)S(1)}, f32[112,128]{1,0:T(8,128)S(1)}, u32[]{:S(2)}, u32[]{:S(2)}) collective-permute-start(f32[112,128]{1,0:T(8,128)S(1)} %get-tuple-element.111), channel_id=1, source_target_pairs={{8,16},{16,8},{9,17},{17,9},{10,18},{18,10},{11,19},{19,11},{12,20... | collective-permute-start | bytes 172040 | tf_op jit(solution)/shard_map/ppermute | solution.py:852
where the time goes:
time: 57.1 us; the launch traced here: 56.3 us
  starting transfers between devices  25.4 us (44%)
  blocking collectives  14.7 us (26%)
  Pallas kernels  9.73 us (17%)
  waiting for transfers between devices  6.3 us (11%)
    ppermute x12, starting transfers between devices, swap(): got[first] = lax.ppermute(pair[first], axis, route)  25.4 us
    all_to_all x1, blocking collectives, body(): lax.all_to_all(message, ('gx', 'gy'), 0, 0).reshape(gx, gy, 16, NL)  14.7 us
    ppermute x12, waiting for transfers between devices, swap(): got[first] = lax.ppermute(pair[first], axis, route)  6.3 us
    pallas_call x1, Pallas kernels, body(): pl.pallas_call(finish_kernel(len(inputs), (gx, gy, wx, wy)), out_shape=sd...  3.62 us
    pallas_call x1, Pallas kernels, body(): call(mid_pre, fields1 + (sds(gx * gy, 16, NL),), [pltpu.VMEM((G1 // 2 * Y...  1.68 us
    pallas_call x1, Pallas kernels, body(): call(pack_y, whole + (sds(8, NL),) + (sds(YROWS + 8, NL),) * 2 + (sds(12...  1.52 us
    pallas_call x1, Pallas kernels, body(): state = call(fine_own, fields)(*args, *halos)  1.41 us
  transfers between devices with their start and end apart: 12, of which 3 were waited for; matrix products, arithmetic and copies ran while one was open for 0% of the time, Pallas kernels for 4%

commit v1 on v0

--- a/solution.py
+++ b/solution.py
@@ -704,15 +704,16 @@
     j4 = lane % 4
     even = (j4 + lane // 4) % 2 == 0
 
-    def around(ref, colour):
-        v = ref[1 - colour]
-        mid = v[1 : wy + 1]
+    def around(ref, colour, b, n):
+        v = ref[1 - colour, pl.ds(b, n + 2)]
+        mid = v[1 : n + 1]
         one, two = rot(mid, 1, 1), rot(mid, -1, 1)
+        mask, j = even[:n], j4[:n]
         return (
             mid,
-            jnp.where(even, one, two) if colour == 0 else jnp.where(even, two, one),
-            jnp.where(j4 < 3, rot(mid, -1, 2), rot(v[2:], 3, 2)),
-            jnp.where(j4 > 0, rot(mid, 1, 2), rot(v[:wy], -3, 2)),
+            jnp.where(mask, one, two) if colour == 0 else jnp.where(mask, two, one),
+            jnp.where(j < 3, rot(mid, -1, 2), rot(v[2:], 3, 2)),
+            jnp.where(j > 0, rot(mid, 1, 2), rot(v[:n], -3, 2)),
             rot(mid, -4, 2), rot(mid, 4, 2),
         )
 
@@ -721,25 +722,24 @@
         outside = (at_first & (sub == 0)) | (~at_first & (sub == rows - 1))
         edges = (None, outside, None, None, lane >= NL - 4, lane < 4)
         mine = p2[colour, 1 : wy + 1]
-        for k, (value, edge) in enumerate(zip(around(p2, colour), edges, strict=True)):
+        for k, (value, edge) in enumerate(zip(around(p2, colour, 0, wy), edges, strict=True)):
             face = F32(0.03125) * (mine + value)
             k2[colour, k] = face if edge is None else jnp.where(edge, F32(0.0), face)
     e2[0, 1 : wy + 1] = r2[0] * d2[0]
 
-    def half2(colour):
-        total = r2[colour]
-        for k, value in enumerate(around(e2, colour)):
-            total = total + k2[colour, k] * value
-        e2[colour, 1 : wy + 1] = total * d2[colour]
-
-    half2(1)
-
-    def sweep2(_, carry):
-        half2(0)
-        half2(1)
-        return carry
-
-    lax.fori_loop(0, 3, sweep2, 0, unroll=True)
+    def half2(colour, b, n):
+        here = pl.ds(b, n)
+        total = r2[colour, here]
+        for k, value in enumerate(around(e2, colour, b, n)):
+            total = total + k2[colour, k, here] * value
+        e2[colour, pl.ds(b + 1, n)] = total * d2[colour, here]
+
+    half2(1, 0, wy)
+    for reach, colours in ((2, (0, 1, 0, 1)), (1, (0, 1))):
+        n = min(2 * reach + 1, wy)
+        start_b = jnp.clip(oy - reach, 0, wy - n)
+        for colour in colours:
+            half2(colour, start_b, n)
 
     s8, l8 = iota((8, NL), 0), iota((8, NL), 1)
     even8 = (l8 % 4 + l8 // 4) % 2 == 0

time: 57.1 us -> 56.9 us (level)
  no operation moved by 1% of the time
where the time goes in v1:
time: 56.9 us; the launch traced here: 56.1 us
  starting transfers between devices  25.4 us (45%)
  blocking collectives  14.7 us (26%)
  Pallas kernels  9.51 us (17%)
  waiting for transfers between devices  6.3 us (11%)
    ppermute x12, starting transfers between devices, swap(): got[first] = lax.ppermute(pair[first], axis, route)  25.4 us
    all_to_all x1, blocking collectives, body(): lax.all_to_all(message, ('gx', 'gy'), 0, 0).reshape(gx, gy, 16, NL)  14.7 us
    ppermute x12, waiting for transfers between devices, swap(): got[first] = lax.ppermute(pair[first], axis, route)  6.3 us
    pallas_call x1, Pallas kernels, body(): pl.pallas_call(finish_kernel(len(inputs), (gx, gy, wx, wy)), out_shape=sd...  3.41 us
    pallas_call x1, Pallas kernels, body(): call(mid_pre, fields1 + (sds(gx * gy, 16, NL),), [pltpu.VMEM((G1 // 2 * Y...  1.68 us
    pallas_call x1, Pallas kernels, body(): call(pack_y, whole + (sds(8, NL),) + (sds(YROWS + 8, NL),) * 2 + (sds(12...  1.52 us
    pallas_call x1, Pallas kernels, body(): state = call(fine_own, fields)(*args, *halos)  1.41 us
  transfers between devices with their start and end apart: 12, of which 3 were waited for; matrix products, arithmetic and copies ran while one was open for 0% of the time, Pallas kernels for 4%

profile of v1, /device:TPU:1, one launch (start us, length us, event | category | flops | bytes accessed | tf_op | source)
XLA Modules:
  0.0 56.1 jit_solution(11023563308283983022)
XLA Ops:
  0.0 1.5 %shard_map.55 = (f32[512,128]{1,0:T(8,128)S(1)}, f32[512,128]{1,0:T(8,128)S(1)}, f32[512,128]{1,0:T(8,128)S(1)}, f32[512,128]{1,0:T(8,128)S(1)}, s32[512,128]{1,...) custom-call(f32[512,128]{1,0:T(8,128)} %bitcast.8, ...), custom_call_target="tpu_custom_call" | custom-call | tf_op jit(solution)/shard_map/pallas_call | solution.py:862
  1.5 2.1 %collective-permute-start = (f32[328,128]{1,0:T(8,128)S(1)}, f32[328,128]{1,0:T(8,128)S(1)}, u32[]{:S(2)}, u32[]{:S(2)}) collective-permute-start(f32[328,128]{1,0:T(8,128)S(1)} %get-tuple-element.77), channel_id=1, source_target_pairs={{0,1},{1,0},{2,3},{3,2},{4,5},{5,4},{6,7},{7,6},{8,9},{9,8},{10,11... | collective-permute-start | bytes 503816 | tf_op jit(solution)/shard_map/ppermute | solution.py:852
  3.6 0.7 %collective-permute-start.1 = (f32[328,128]{1,0:T(8,128)S(1)}, f32[328,128]{1,0:T(8,128)S(1)}, u32[]{:S(2)}, u32[]{:S(2)}) collective-permute-start(f32[328,128]{1,0:T(8,128)S(1)} %get-tuple-element.78), channel_id=1, source_target_pairs={{1,2},{2,1},{3,4},{4,3},{5,6},{6,5},{9,10},{10,9},{11,12},{12,11},... | collective-permute-start | bytes 503816 | tf_op jit(solution)/shard_map/ppermute | solution.py:852
  4.3 1.0 %collective-permute-start.2 = (f32[192,128]{1,0:T(8,128)S(1)}, f32[192,128]{1,0:T(8,128)S(1)}, u32[]{:S(2)}, u32[]{:S(2)}) collective-permute-start(f32[192,128]{1,0:T(8,128)S(1)} %get-tuple-element.79), channel_id=1, source_target_pairs={{0,8},{8,0},{16,24},{24,16},{1,9},{9,1},{17,25},{25,17},{2,10},{10... | collective-permute-start | bytes 294920 | tf_op jit(solution)/shard_map/ppermute | solution.py:852
  5.3 3.0 %collective-permute-start.3 = (f32[192,128]{1,0:T(8,128)S(1)}, f32[192,128]{1,0:T(8,128)S(1)}, u32[]{:S(2)}, u32[]{:S(2)}) collective-permute-start(f32[192,128]{1,0:T(8,128)S(1)} %get-tuple-element.80), channel_id=1, source_target_pairs={{8,16},{16,8},{9,17},{17,9},{10,18},{18,10},{11,19},{19,11},{12,20... | collective-permute-start | bytes 294920 | tf_op jit(solution)/shard_map/ppermute | solution.py:852
  8.4 0.0 collective-permute-done.got0.goty0.refs_2_
  8.4 0.0 collective-permute-done.1.got1.goty1.refs_3_
  8.4 0.2 shard_map.56
  8.6 3.4 %collective-permute-start.4 = (f32[120,128]{1,0:T(8,128)S(1)}, f32[120,128]{1,0:T(8,128)S(1)}, u32[]{:S(2)}, u32[]{:S(2)}) collective-permute-start(f32[120,128]{1,0:T(8,128)S(1)} %get-tuple-element.82), channel_id=1, source_target_pairs={{0,8},{8,0},{16,24},{24,16},{1,9},{9,1},{17,25},{25,17},{2,10},{10... | collective-permute-start | bytes 184328 | tf_op jit(solution)/shard_map/ppermute | solution.py:852
  12.0 3.0 %collective-permute-start.5 = (f32[120,128]{1,0:T(8,128)S(1)}, f32[120,128]{1,0:T(8,128)S(1)}, u32[]{:S(2)}, u32[]{:S(2)}) collective-permute-start(f32[120,128]{1,0:T(8,128)S(1)} %get-tuple-element.83), channel_id=1, source_target_pairs={{8,16},{16,8},{9,17},{17,9},{10,18},{18,10},{11,19},{19,11},{12,20... | collective-permute-start | bytes 184328 | tf_op jit(solution)/shard_map/ppermute | solution.py:852
  15.1 1.4 %shard_map.57 = (f32[2,20,24,128]{3,2,1,0:T(8,128)S(1)}, f32[2,20,24,128]{3,2,1,0:T(8,128)S(1)}, f32[2,20,24,128]{3,2,1,0:T(8,128)S(1)}, f32[20,24,128]{2,1,0:T(...) custom-call(f32[512,128]{1,0:T(8,128)S(1)} %get-tuple-element.84.pot, ...), custom_call_target="tpu_custom_call" | custom-call | tf_op jit(solution)/shard_map/pallas_call | solution.py:877
  16.5 0.0 collective-permute-done.2.xm0
  16.5 0.0 collective-permute-done.3.xm1
  16.5 0.0 collective-permute-done.4.got0.fx0.refs_4_
  16.5 1.0 %collective-permute-done.5.got1.fx1.refs_5_ = f32[120,128]{1,0:T(8,128)S(1)} collective-permute-done((f32[120,128]{1,0:T(8,128)S(1)}, f32[120,128]{1,0:T(8,128)S(1)}, u32[]{:S(2)}, u32[]{:S(2)}) %collective-permute-start.5) | collective-permute-done | bytes 61472 | tf_op jit(solution)/shard_map/ppermute | solution.py:852
  17.5 0.9 %shard_map.58 = (f32[2,20,24,128]{3,2,1,0:T(8,128)S(1)}, f32[2,20,24,128]{3,2,1,0:T(8,128)S(1)}, f32[2,20,24,128]{3,2,1,0:T(8,128)S(1)}, f32[20,24,128]{2,1,0:T(...) custom-call(f32[328,128]{1,0:T(8,128)S(1)} %collective-permute-done., ...), custom_call_target="tpu_custom_call", output_to_operand_aliasing={{0}: (6, {}), {1}: (7, {}), {2}: (8, {}), {3}: (9, {}), {4}... | custom-call | tf_op jit(solution)/shard_map/pallas_call | solution.py:878
  18.4 0.7 %collective-permute-start.9 = (f32[216,128]{1,0:T(8,128)S(1)}, f32[216,128]{1,0:T(8,128)S(1)}, u32[]{:S(2)}, u32[]{:S(2)}) collective-permute-start(f32[216,128]{1,0:T(8,128)S(1)} %get-tuple-element.113), channel_id=1, source_target_pairs={{1,2},{2,1},{3,4},{4,3},{5,6},{6,5},{9,10},{10,9},{11,12},{12,11},... | collective-permute-start | bytes 331784 | tf_op jit(solution)/shard_map/ppermute | solution.py:852
  19.1 5.1 %collective-permute-start.8 = (f32[216,128]{1,0:T(8,128)S(1)}, f32[216,128]{1,0:T(8,128)S(1)}, u32[]{:S(2)}, u32[]{:S(2)}) collective-permute-start(f32[216,128]{1,0:T(8,128)S(1)} %get-tuple-element.112.m0), channel_id=1, source_target_pairs={{0,1},{1,0},{2,3},{3,2},{4,5},{5,4},{6,7},{7,6},{8,9},{9,8},{10,11... | collective-permute-start | bytes 331784 | tf_op jit(solution)/shard_map/ppermute | solution.py:852
  24.2 0.0 collective-permute-done.9.got1.gy1.refs_27_
  24.2 2.1 %collective-permute-done.8.got0.gy0.refs_26_ = f32[216,128]{1,0:T(8,128)S(1)} collective-permute-done((f32[216,128]{1,0:T(8,128)S(1)}, f32[216,128]{1,0:T(8,128)S(1)}, u32[]{:S(2)}, u32[]{:S(2)}) %collective-permute-start.8) | collective-permute-done | bytes 110624 | tf_op jit(solution)/shard_map/ppermute | solution.py:852
  26.4 0.1 collective-permute-start.10
  26.5 4.2 %collective-permute-start.11 = (f32[184,128]{1,0:T(8,128)S(1)}, f32[184,128]{1,0:T(8,128)S(1)}, u32[]{:S(2)}, u32[]{:S(2)}) collective-permute-start(f32[184,128]{1,0:T(8,128)S(1)} %get-tuple-element.115), channel_id=1, source_target_pairs={{8,16},{16,8},{9,17},{17,9},{10,18},{18,10},{11,19},{19,11},{12,20... | collective-permute-start | bytes 282632 | tf_op jit(solution)/shard_map/ppermute | solution.py:852
  30.7 0.1 collective-permute-start.6
  30.8 1.9 %collective-permute-start.7 = (f32[112,128]{1,0:T(8,128)S(1)}, f32[112,128]{1,0:T(8,128)S(1)}, u32[]{:S(2)}, u32[]{:S(2)}) collective-permute-start(f32[112,128]{1,0:T(8,128)S(1)} %get-tuple-element.111), channel_id=1, source_target_pairs={{8,16},{16,8},{9,17},{17,9},{10,18},{18,10},{11,19},{19,11},{12,20... | collective-permute-start | bytes 172040 | tf_op jit(solution)/shard_map/ppermute | solution.py:852
  32.7 0.4 shard_map.60
  33.1 0.0 collective-permute-done.6.xm0.refs_28_
  33.1 3.1 %collective-permute-done.7.xm1.refs_29_ = f32[112,128]{1,0:T(8,128)S(1)} collective-permute-done((f32[112,128]{1,0:T(8,128)S(1)}, f32[112,128]{1,0:T(8,128)S(1)}, u32[]{:S(2)}, u32[]{:S(2)}) %collective-permute-start.7) | collective-permute-done | bytes 57376 | tf_op jit(solution)/shard_map/ppermute | solution.py:852
  36.3 0.0 collective-permute-done.10.gx0.refs_30_
  36.3 0.0 collective-permute-done.11.gx1.refs_31_
  36.3 1.7 %shard_map.61 = (f32[2,18,24,128]{3,2,1,0:T(8,128)S(1)}, f32[2,18,24,128]{3,2,1,0:T(8,128)S(1)}, f32[2,18,24,128]{3,2,1,0:T(8,128)S(1)}, f32[2,18,24,128]{3,2,1,...) custom-call(f32[112,128]{1,0:T(8,128)S(1)} %collective-permute-done., ...), custom_call_target="tpu_custom_call", output_to_operand_aliasing={{0}: (6, {}), {1}: (7, {}), {2}: (8, {}), {3}: (9, {}), {4}... | custom-call | tf_op jit(solution)/shard_map/pallas_call | solution.py:892
  37.9 14.7 %all_to_all.5 = f32[32,16,128]{2,1,0:T(8,128)S(1)} all-to-all(f32[32,16,128]{2,1,0:T(8,128)S(1)} %get-tuple-element.128), channel_id=1, replica_groups=mesh['gx'=4,'gy'=8] {'gx','gy'}, dimensions={0} | all-to-all | bytes 524288 | tf_op jit(solution)/shard_map/all_to_all | solution.py:906
  52.7 3.4 %finish.1 = f32[512,128]{1,0:T(8,128)} custom-call(f32[4,8,16,128]{3,2,1,0:T(8,128)S(1)} %bitcast.7, f32[8,128]{1,0:T(8,128)S(1)} %get-tuple-element.81.p2.refs_1_, f32[328,128]{1,0:T(8,128)S(1)} %collective-permute-done.got0.goty0.refs_2_, f32[328,128]{1,0:T(8,128)S(1)} %collective-permute-done.1.got1.goty1.refs_3_, ...), custom_call_target="tpu_custom_call" | custom-call | tf_op jit(solution)/shard_map/finish/pallas_call | solution.py:913
  (1 shorter events, 0.0 us)
Async XLA Ops:
  1.5 6.8 %collective-permute-start = (f32[328,128]{1,0:T(8,128)S(1)}, f32[328,128]{1,0:T(8,128)S(1)}, u32[]{:S(2)}, u32[]{:S(2)}) collective-permute-start(f32[328,128]{1,0:T(8,128)S(1)} %get-tuple-element.77), channel_id=1, source_target_pairs={{0,1},{1,0},{2,3},{3,2},{4,5},{5,4},{6,7},{7,6},{8,9},{9,8},{10,11... | collective-permute-start | bytes 503816 | tf_op jit(solution)/shard_map/ppermute | solution.py:852
  3.6 4.8 %collective-permute-start.1 = (f32[328,128]{1,0:T(8,128)S(1)}, f32[328,128]{1,0:T(8,128)S(1)}, u32[]{:S(2)}, u32[]{:S(2)}) collective-permute-start(f32[328,128]{1,0:T(8,128)S(1)} %get-tuple-element.78), channel_id=1, source_target_pairs={{1,2},{2,1},{3,4},{4,3},{5,6},{6,5},{9,10},{10,9},{11,12},{12,11},... | collective-permute-start | bytes 503816 | tf_op jit(solution)/shard_map/ppermute | solution.py:852
  4.3 12.2 %collective-permute-start.2 = (f32[192,128]{1,0:T(8,128)S(1)}, f32[192,128]{1,0:T(8,128)S(1)}, u32[]{:S(2)}, u32[]{:S(2)}) collective-permute-start(f32[192,128]{1,0:T(8,128)S(1)} %get-tuple-element.79), channel_id=1, source_target_pairs={{0,8},{8,0},{16,24},{24,16},{1,9},{9,1},{17,25},{25,17},{2,10},{10... | collective-permute-start | bytes 294920 | tf_op jit(solution)/shard_map/ppermute | solution.py:852
  5.3 11.2 %collective-permute-start.3 = (f32[192,128]{1,0:T(8,128)S(1)}, f32[192,128]{1,0:T(8,128)S(1)}, u32[]{:S(2)}, u32[]{:S(2)}) collective-permute-start(f32[192,128]{1,0:T(8,128)S(1)} %get-tuple-element.80), channel_id=1, source_target_pairs={{8,16},{16,8},{9,17},{17,9},{10,18},{18,10},{11,19},{19,11},{12,20... | collective-permute-start | bytes 294920 | tf_op jit(solution)/shard_map/ppermute | solution.py:852
  8.6 7.9 %collective-permute-start.4 = (f32[120,128]{1,0:T(8,128)S(1)}, f32[120,128]{1,0:T(8,128)S(1)}, u32[]{:S(2)}, u32[]{:S(2)}) collective-permute-start(f32[120,128]{1,0:T(8,128)S(1)} %get-tuple-element.82), channel_id=1, source_target_pairs={{0,8},{8,0},{16,24},{24,16},{1,9},{9,1},{17,25},{25,17},{2,10},{10... | collective-permute-start | bytes 184328 | tf_op jit(solution)/shard_map/ppermute | solution.py:852
  12.0 5.5 %collective-permute-start.5 = (f32[120,128]{1,0:T(8,128)S(1)}, f32[120,128]{1,0:T(8,128)S(1)}, u32[]{:S(2)}, u32[]{:S(2)}) collective-permute-start(f32[120,128]{1,0:T(8,128)S(1)} %get-tuple-element.83), channel_id=1, source_target_pairs={{8,16},{16,8},{9,17},{17,9},{10,18},{18,10},{11,19},{19,11},{12,20... | collective-permute-start | bytes 184328 | tf_op jit(solution)/shard_map/ppermute | solution.py:852
  18.4 5.8 %collective-permute-start.9 = (f32[216,128]{1,0:T(8,128)S(1)}, f32[216,128]{1,0:T(8,128)S(1)}, u32[]{:S(2)}, u32[]{:S(2)}) collective-permute-start(f32[216,128]{1,0:T(8,128)S(1)} %get-tuple-element.113), channel_id=1, source_target_pairs={{1,2},{2,1},{3,4},{4,3},{5,6},{6,5},{9,10},{10,9},{11,12},{12,11},... | collective-permute-start | bytes 331784 | tf_op jit(solution)/shard_map/ppermute | solution.py:852
  19.1 7.3 %collective-permute-start.8 = (f32[216,128]{1,0:T(8,128)S(1)}, f32[216,128]{1,0:T(8,128)S(1)}, u32[]{:S(2)}, u32[]{:S(2)}) collective-permute-start(f32[216,128]{1,0:T(8,128)S(1)} %get-tuple-element.112.m0), channel_id=1, source_target_pairs={{0,1},{1,0},{2,3},{3,2},{4,5},{5,4},{6,7},{7,6},{8,9},{9,8},{10,11... | collective-permute-start | bytes 331784 | tf_op jit(solution)/shard_map/ppermute | solution.py:852
  26.4 9.9 %collective-permute-start.10 = (f32[184,128]{1,0:T(8,128)S(1)}, f32[184,128]{1,0:T(8,128)S(1)}, u32[]{:S(2)}, u32[]{:S(2)}) collective-permute-start(f32[184,128]{1,0:T(8,128)S(1)} %get-tuple-element.114), channel_id=1, source_target_pairs={{0,8},{8,0},{16,24},{24,16},{1,9},{9,1},{17,25},{25,17},{2,10},{10... | collective-permute-start | bytes 282632 | tf_op jit(solution)/shard_map/ppermute | solution.py:852
  26.5 9.8 %collective-permute-start.11 = (f32[184,128]{1,0:T(8,128)S(1)}, f32[184,128]{1,0:T(8,128)S(1)}, u32[]{:S(2)}, u32[]{:S(2)}) collective-permute-start(f32[184,128]{1,0:T(8,128)S(1)} %get-tuple-element.115), channel_id=1, source_target_pairs={{8,16},{16,8},{9,17},{17,9},{10,18},{18,10},{11,19},{19,11},{12,20... | collective-permute-start | bytes 282632 | tf_op jit(solution)/shard_map/ppermute | solution.py:852
  30.7 2.5 %collective-permute-start.6 = (f32[112,128]{1,0:T(8,128)S(1)}, f32[112,128]{1,0:T(8,128)S(1)}, u32[]{:S(2)}, u32[]{:S(2)}) collective-permute-start(f32[112,128]{1,0:T(8,128)S(1)} %get-tuple-element.110), channel_id=1, source_target_pairs={{0,8},{8,0},{16,24},{24,16},{1,9},{9,1},{17,25},{25,17},{2,10},{10... | collective-permute-start | bytes 172040 | tf_op jit(solution)/shard_map/ppermute | solution.py:852
  30.8 5.5 %collective-permute-start.7 = (f32[112,128]{1,0:T(8,128)S(1)}, f32[112,128]{1,0:T(8,128)S(1)}, u32[]{:S(2)}, u32[]{:S(2)}) collective-permute-start(f32[112,128]{1,0:T(8,128)S(1)} %get-tuple-element.111), channel_id=1, source_target_pairs={{8,16},{16,8},{9,17},{17,9},{10,18},{18,10},{11,19},{19,11},{12,20... | collective-permute-start | bytes 172040 | tf_op jit(solution)/shard_map/ppermute | solution.py:852

commit v2 on v1

--- a/solution.py
+++ b/solution.py
@@ -15,7 +15,6 @@
 NM = G1 // 2 + 2
 STATE = 16
 GF = 3
-GM = 8
 LN2 = 0.6931471805599453
 
 
@@ -503,7 +502,7 @@
     return jnp.where(lane % 2 == 1, value, rot(value, -1, value.ndim - 1))
 
 
-MIDS = 10
+MIDS = 12
 
 
 def mid_put(state, k, rows, one, two, both):
@@ -520,15 +519,15 @@
 
 
 def mid_begin(state, at, n):
-    e, r, d, p, *faces = state
+    e, r, d, p, *faces = state[:10]
     here = pl.ds(at, n)
     faces_of(p, at, n, 0.25, 2, *faces)
     e[0, here] = r[0, here] * d[0, here]
 
 
-def mid_own(m0, gy0, gy1, *state):
+def mid_own(m0, gy0, gy1, csum, *state):
     gys = (gy0, gy1)
-    e, r, d, p, *faces = state
+    e, r, d, p, *faces, t, tc = state
 
     def own(hi, lo):
         for k in range(X1 // 2):
@@ -541,14 +540,20 @@
     first = 2 + H1 // 2
     groups(first, X1 // 2 - 2, 2, lambda at: mid_begin(state, at, 2))
     groups(first + 1, X1 // 2 - 4, 2, lambda at: coarse_half(e, r, d, at, 2, 1, faces, 2))
+    for x2 in range(H1 // 2, H1 // 2 + X1 // 2):
+        mid_coarse_p(p, t, x2)
+    tc[...] = lane_pairs(csum[...], 2).reshape(X1 // 2 * 8, NL)
+
+
+def mid_coarse_p(p, t, x2):
+    t[x2 * YE : (x2 + 1) * YE, :] = lane_pairs(p[0, x2 + 1] + p[1, x2 + 1], 2)
 
 
 def mid_pre(xm0, xm1, gx0, gx1, csum, g1, *refs_):
     gxs, mains = (gx0, gx1), (xm0, xm1)
     state, refs_ = refs_[MIDS : 2 * MIDS], refs_[2 * MIDS :]
-    e, r, d, p, *faces = state
-    fin, fout, fyp, fym, fzp, fzm = faces
-    msg, t, tr, tc, pc, pk = refs_
+    e, r, d, p, *faces, t, tc = state
+    msg, tr, pc, pk = refs_
 
     def beyond(main, ref, at, far):
         def whole(row, start, count):
@@ -577,7 +582,7 @@
     for at in (1, inner + X1 // 2 - 2):
         coarse_half(e, r, d, at, inner + 1, 1, faces, 2)
     for colour in (0, 1):
-        groups(1, NM - 2, GM, lambda at, colour=colour: coarse_half(e, r, d, at, GM, colour, faces, 2))
+        groups(2, NM - 4, 7, lambda at, colour=colour: coarse_half(e, r, d, at, 7, colour, faces, 2))
 
     def down(at):
         n = 4
@@ -589,15 +594,11 @@
             left += part[:, 0:8] - g1[colour, k] * e[colour, here, 0:8, :]
         to = pl.multiple_of((at - 1 - H1 // 2) * 8, 8)
         tr[pl.ds(to, n * 8), :] = lane_pairs(left, 2).reshape(n * 8, NL)
-        tc[pl.ds(to, n * 8), :] = lane_pairs(csum[k], 2).reshape(n * 8, NL)
 
     groups(1 + H1 // 2, X1 // 2, 4, down)
 
-    def coarse_p(x2, _):
-        t[pl.ds(pl.multiple_of(x2 * YE, 8), YE), :] = lane_pairs(p[0, x2 + 1] + p[1, x2 + 1], 2)
-        return 0
-
-    lax.fori_loop(0, G1 // 2, coarse_p, 0, unroll=4)
+    for x2 in (*range(H1 // 2), *range(H1 // 2 + X1 // 2, G1 // 2)):
+        mid_coarse_p(p, t, x2)
 
     eighth = F32(0.125)
     n2, m2 = X1 // 2, G1 // 2
@@ -888,20 +889,19 @@
 
     mid, mid1 = (2, NM, YE, NL), (NM, YE, NL)
     fields1 = (sds(*mid),) * 4 + (sds(*mid1),) + (sds(*mid),) * 5
-    level1 = call(mid_own, fields1)(m0, *goty1)
+    fields1 += (sds(G1 // 2 * YE, NL), sds(X1 // 2 * 8, NL))
+    level1 = call(mid_own, fields1)(m0, *goty1, c1)
     *level1, message = call(
         mid_pre,
         fields1 + (sds(gx * gy, 16, NL),),
         [
-            pltpu.VMEM((G1 // 2 * YE, NL), F32),
-            pltpu.VMEM((X1 // 2 * 8, NL), F32),
             pltpu.VMEM((X1 // 2 * 8, NL), F32),
             pltpu.VMEM((3, G1 // 2, NL), F32),
             pltpu.VMEM((24, NL), F32),
         ],
         alias={6 + k: k for k in range(MIDS)},
     )(*xm1, *gotx1, c1, g1, *level1)
-    level1 = (*level1[:3], *level1[4:])
+    level1 = (*level1[:3], *level1[4:10])
 
     gathered = lax.all_to_all(message, ("gx", "gy"), 0, 0).reshape(gx, gy, 16, NL)
     wx, wy = min(gx, 6), min(gy, 8)

time: 56.9 us -> 56.4 us (level)
  no operation moved by 1% of the time
where the time goes in v2:
time: 56.4 us; the launch traced here: 55.6 us
  starting transfers between devices  25.4 us (45%)
  blocking collectives  14.7 us (26%)
  Pallas kernels  9.08 us (16%)
  waiting for transfers between devices  6.25 us (11%)
    ppermute x12, starting transfers between devices, swap(): got[first] = lax.ppermute(pair[first], axis, route)  25.4 us
    all_to_all x1, blocking collectives, body(): lax.all_to_all(message, ('gx', 'gy'), 0, 0).reshape(gx, gy, 16, NL)  14.7 us
    ppermute x12, waiting for transfers between devices, swap(): got[first] = lax.ppermute(pair[first], axis, route)  6.25 us
    pallas_call x1, Pallas kernels, body(): pl.pallas_call(finish_kernel(len(inputs), (gx, gy, wx, wy)), out_shape=sd...  3.41 us
    pallas_call x1, Pallas kernels, body(): call(pack_y, whole + (sds(8, NL),) + (sds(YROWS + 8, NL),) * 2 + (sds(12...  1.52 us
    pallas_call x1, Pallas kernels, body(): state = call(fine_own, fields)(*args, *halos)  1.4 us
    pallas_call x1, Pallas kernels, body(): call(mid_pre, fields1 + (sds(gx * gy, 16, NL),), [pltpu.VMEM((X1 // 2 * 8...  1.2 us
  transfers between devices with their start and end apart: 12, of which 3 were waited for; matrix products, arithmetic and copies ran while one was open for 0% of the time, Pallas kernels for 4%

profile of v2, /device:TPU:1, one launch (start us, length us, event | category | flops | bytes accessed | tf_op | source)
XLA Modules:
  0.0 55.6 jit_solution(17565816885033334021)
XLA Ops:
  0.0 1.5 %shard_map.55 = (f32[512,128]{1,0:T(8,128)S(1)}, f32[512,128]{1,0:T(8,128)S(1)}, f32[512,128]{1,0:T(8,128)S(1)}, f32[512,128]{1,0:T(8,128)S(1)}, s32[512,128]{1,...) custom-call(f32[512,128]{1,0:T(8,128)} %bitcast.8, ...), custom_call_target="tpu_custom_call" | custom-call | tf_op jit(solution)/shard_map/pallas_call | solution.py:863
  1.5 2.1 %collective-permute-start = (f32[328,128]{1,0:T(8,128)S(1)}, f32[328,128]{1,0:T(8,128)S(1)}, u32[]{:S(2)}, u32[]{:S(2)}) collective-permute-start(f32[328,128]{1,0:T(8,128)S(1)} %get-tuple-element.79), channel_id=1, source_target_pairs={{0,1},{1,0},{2,3},{3,2},{4,5},{5,4},{6,7},{7,6},{8,9},{9,8},{10,11... | collective-permute-start | bytes 503816 | tf_op jit(solution)/shard_map/ppermute | solution.py:853
  3.6 0.7 %collective-permute-start.1 = (f32[328,128]{1,0:T(8,128)S(1)}, f32[328,128]{1,0:T(8,128)S(1)}, u32[]{:S(2)}, u32[]{:S(2)}) collective-permute-start(f32[328,128]{1,0:T(8,128)S(1)} %get-tuple-element.80), channel_id=1, source_target_pairs={{1,2},{2,1},{3,4},{4,3},{5,6},{6,5},{9,10},{10,9},{11,12},{12,11},... | collective-permute-start | bytes 503816 | tf_op jit(solution)/shard_map/ppermute | solution.py:853
  4.3 1.0 %collective-permute-start.2 = (f32[192,128]{1,0:T(8,128)S(1)}, f32[192,128]{1,0:T(8,128)S(1)}, u32[]{:S(2)}, u32[]{:S(2)}) collective-permute-start(f32[192,128]{1,0:T(8,128)S(1)} %get-tuple-element.81), channel_id=1, source_target_pairs={{0,8},{8,0},{16,24},{24,16},{1,9},{9,1},{17,25},{25,17},{2,10},{10... | collective-permute-start | bytes 294920 | tf_op jit(solution)/shard_map/ppermute | solution.py:853
  5.3 3.0 %collective-permute-start.3 = (f32[192,128]{1,0:T(8,128)S(1)}, f32[192,128]{1,0:T(8,128)S(1)}, u32[]{:S(2)}, u32[]{:S(2)}) collective-permute-start(f32[192,128]{1,0:T(8,128)S(1)} %get-tuple-element.82), channel_id=1, source_target_pairs={{8,16},{16,8},{9,17},{17,9},{10,18},{18,10},{11,19},{19,11},{12,20... | collective-permute-start | bytes 294920 | tf_op jit(solution)/shard_map/ppermute | solution.py:853
  8.4 0.0 collective-permute-done.got0.goty0.refs_2_
  8.4 0.0 collective-permute-done.1.got1.goty1.refs_3_
  8.4 0.2 shard_map.56
  8.6 3.4 %collective-permute-start.4 = (f32[120,128]{1,0:T(8,128)S(1)}, f32[120,128]{1,0:T(8,128)S(1)}, u32[]{:S(2)}, u32[]{:S(2)}) collective-permute-start(f32[120,128]{1,0:T(8,128)S(1)} %get-tuple-element.84), channel_id=1, source_target_pairs={{0,8},{8,0},{16,24},{24,16},{1,9},{9,1},{17,25},{25,17},{2,10},{10... | collective-permute-start | bytes 184328 | tf_op jit(solution)/shard_map/ppermute | solution.py:853
  12.0 3.0 %collective-permute-start.5 = (f32[120,128]{1,0:T(8,128)S(1)}, f32[120,128]{1,0:T(8,128)S(1)}, u32[]{:S(2)}, u32[]{:S(2)}) collective-permute-start(f32[120,128]{1,0:T(8,128)S(1)} %get-tuple-element.85), channel_id=1, source_target_pairs={{8,16},{16,8},{9,17},{17,9},{10,18},{18,10},{11,19},{19,11},{12,20... | collective-permute-start | bytes 184328 | tf_op jit(solution)/shard_map/ppermute | solution.py:853
  15.1 1.4 %shard_map.57 = (f32[2,20,24,128]{3,2,1,0:T(8,128)S(1)}, f32[2,20,24,128]{3,2,1,0:T(8,128)S(1)}, f32[2,20,24,128]{3,2,1,0:T(8,128)S(1)}, f32[20,24,128]{2,1,0:T(...) custom-call(f32[512,128]{1,0:T(8,128)S(1)} %get-tuple-element.86.pot, ...), custom_call_target="tpu_custom_call" | custom-call | tf_op jit(solution)/shard_map/pallas_call | solution.py:878
  16.5 0.0 collective-permute-done.2.xm0
  16.5 0.0 collective-permute-done.3.xm1
  16.5 0.0 collective-permute-done.4.got0.fx0.refs_4_
  16.5 1.0 %collective-permute-done.5.got1.fx1.refs_5_ = f32[120,128]{1,0:T(8,128)S(1)} collective-permute-done((f32[120,128]{1,0:T(8,128)S(1)}, f32[120,128]{1,0:T(8,128)S(1)}, u32[]{:S(2)}, u32[]{:S(2)}) %collective-permute-start.5) | collective-permute-done | bytes 61472 | tf_op jit(solution)/shard_map/ppermute | solution.py:853
  17.5 0.9 %shard_map.58 = (f32[2,20,24,128]{3,2,1,0:T(8,128)S(1)}, f32[2,20,24,128]{3,2,1,0:T(8,128)S(1)}, f32[2,20,24,128]{3,2,1,0:T(8,128)S(1)}, f32[20,24,128]{2,1,0:T(...) custom-call(f32[328,128]{1,0:T(8,128)S(1)} %collective-permute-done., ...), custom_call_target="tpu_custom_call", output_to_operand_aliasing={{0}: (6, {}), {1}: (7, {}), {2}: (8, {}), {3}: (9, {}), {4}... | custom-call | tf_op jit(solution)/shard_map/pallas_call | solution.py:879
  18.4 0.7 %collective-permute-start.9 = (f32[216,128]{1,0:T(8,128)S(1)}, f32[216,128]{1,0:T(8,128)S(1)}, u32[]{:S(2)}, u32[]{:S(2)}) collective-permute-start(f32[216,128]{1,0:T(8,128)S(1)} %get-tuple-element.115), channel_id=1, source_target_pairs={{1,2},{2,1},{3,4},{4,3},{5,6},{6,5},{9,10},{10,9},{11,12},{12,11},... | collective-permute-start | bytes 331784 | tf_op jit(solution)/shard_map/ppermute | solution.py:853
  19.1 5.1 %collective-permute-start.8 = (f32[216,128]{1,0:T(8,128)S(1)}, f32[216,128]{1,0:T(8,128)S(1)}, u32[]{:S(2)}, u32[]{:S(2)}) collective-permute-start(f32[216,128]{1,0:T(8,128)S(1)} %get-tuple-element.114.m0), channel_id=1, source_target_pairs={{0,1},{1,0},{2,3},{3,2},{4,5},{5,4},{6,7},{7,6},{8,9},{9,8},{10,11... | collective-permute-start | bytes 331784 | tf_op jit(solution)/shard_map/ppermute | solution.py:853
  24.2 0.0 collective-permute-done.9.got1.gy1.refs_27_
  24.2 2.1 %collective-permute-done.8.got0.gy0.refs_26_ = f32[216,128]{1,0:T(8,128)S(1)} collective-permute-done((f32[216,128]{1,0:T(8,128)S(1)}, f32[216,128]{1,0:T(8,128)S(1)}, u32[]{:S(2)}, u32[]{:S(2)}) %collective-permute-start.8) | collective-permute-done | bytes 110624 | tf_op jit(solution)/shard_map/ppermute | solution.py:853
  26.4 0.1 collective-permute-start.10
  26.5 4.2 %collective-permute-start.11 = (f32[184,128]{1,0:T(8,128)S(1)}, f32[184,128]{1,0:T(8,128)S(1)}, u32[]{:S(2)}, u32[]{:S(2)}) collective-permute-start(f32[184,128]{1,0:T(8,128)S(1)} %get-tuple-element.117), channel_id=1, source_target_pairs={{8,16},{16,8},{9,17},{17,9},{10,18},{18,10},{11,19},{19,11},{12,20... | collective-permute-start | bytes 282632 | tf_op jit(solution)/shard_map/ppermute | solution.py:853
  30.7 0.1 collective-permute-start.6
  30.8 1.9 %collective-permute-start.7 = (f32[112,128]{1,0:T(8,128)S(1)}, f32[112,128]{1,0:T(8,128)S(1)}, u32[]{:S(2)}, u32[]{:S(2)}) collective-permute-start(f32[112,128]{1,0:T(8,128)S(1)} %get-tuple-element.113), channel_id=1, source_target_pairs={{8,16},{16,8},{9,17},{17,9},{10,18},{18,10},{11,19},{19,11},{12,20... | collective-permute-start | bytes 172040 | tf_op jit(solution)/shard_map/ppermute | solution.py:853
  32.7 0.5 shard_map.60
  33.2 0.0 collective-permute-done.6.xm0.refs_28_
  33.2 3.1 %collective-permute-done.7.xm1.refs_29_ = f32[112,128]{1,0:T(8,128)S(1)} collective-permute-done((f32[112,128]{1,0:T(8,128)S(1)}, f32[112,128]{1,0:T(8,128)S(1)}, u32[]{:S(2)}, u32[]{:S(2)}) %collective-permute-start.7) | collective-permute-done | bytes 57376 | tf_op jit(solution)/shard_map/ppermute | solution.py:853
  36.3 0.0 collective-permute-done.10.gx0.refs_30_
  36.3 0.0 collective-permute-done.11.gx1.refs_31_
  36.3 1.2 %shard_map.61 = (f32[2,18,24,128]{3,2,1,0:T(8,128)S(1)}, f32[2,18,24,128]{3,2,1,0:T(8,128)S(1)}, f32[2,18,24,128]{3,2,1,0:T(8,128)S(1)}, f32[2,18,24,128]{3,2,1,...) custom-call(f32[112,128]{1,0:T(8,128)S(1)} %collective-permute-done., ...), custom_call_target="tpu_custom_call", output_to_operand_aliasing={{0}: (6, {}), {1}: (7, {}), {2}: (8, {}), {3}: (9, {}), {4}... | custom-call | tf_op jit(solution)/shard_map/pallas_call | solution.py:894
  37.5 14.7 %all_to_all.5 = f32[32,16,128]{2,1,0:T(8,128)S(1)} all-to-all(f32[32,16,128]{2,1,0:T(8,128)S(1)} %get-tuple-element.132), channel_id=1, replica_groups=mesh['gx'=4,'gy'=8] {'gx','gy'}, dimensions={0} | all-to-all | bytes 524288 | tf_op jit(solution)/shard_map/all_to_all | solution.py:906
  52.2 3.4 %finish.1 = f32[512,128]{1,0:T(8,128)} custom-call(f32[4,8,16,128]{3,2,1,0:T(8,128)S(1)} %bitcast.7, f32[8,128]{1,0:T(8,128)S(1)} %get-tuple-element.83.p2.refs_1_, f32[328,128]{1,0:T(8,128)S(1)} %collective-permute-done.got0.goty0.refs_2_, f32[328,128]{1,0:T(8,128)S(1)} %collective-permute-done.1.got1.goty1.refs_3_, ...), custom_call_target="tpu_custom_call" | custom-call | tf_op jit(solution)/shard_map/finish/pallas_call | solution.py:913
  (1 shorter events, 0.0 us)
Async XLA Ops:
  1.5 6.8 %collective-permute-start = (f32[328,128]{1,0:T(8,128)S(1)}, f32[328,128]{1,0:T(8,128)S(1)}, u32[]{:S(2)}, u32[]{:S(2)}) collective-permute-start(f32[328,128]{1,0:T(8,128)S(1)} %get-tuple-element.79), channel_id=1, source_target_pairs={{0,1},{1,0},{2,3},{3,2},{4,5},{5,4},{6,7},{7,6},{8,9},{9,8},{10,11... | collective-permute-start | bytes 503816 | tf_op jit(solution)/shard_map/ppermute | solution.py:853
  3.6 4.8 %collective-permute-start.1 = (f32[328,128]{1,0:T(8,128)S(1)}, f32[328,128]{1,0:T(8,128)S(1)}, u32[]{:S(2)}, u32[]{:S(2)}) collective-permute-start(f32[328,128]{1,0:T(8,128)S(1)} %get-tuple-element.80), channel_id=1, source_target_pairs={{1,2},{2,1},{3,4},{4,3},{5,6},{6,5},{9,10},{10,9},{11,12},{12,11},... | collective-permute-start | bytes 503816 | tf_op jit(solution)/shard_map/ppermute | solution.py:853
  4.3 12.2 %collective-permute-start.2 = (f32[192,128]{1,0:T(8,128)S(1)}, f32[192,128]{1,0:T(8,128)S(1)}, u32[]{:S(2)}, u32[]{:S(2)}) collective-permute-start(f32[192,128]{1,0:T(8,128)S(1)} %get-tuple-element.81), channel_id=1, source_target_pairs={{0,8},{8,0},{16,24},{24,16},{1,9},{9,1},{17,25},{25,17},{2,10},{10... | collective-permute-start | bytes 294920 | tf_op jit(solution)/shard_map/ppermute | solution.py:853
  5.3 11.2 %collective-permute-start.3 = (f32[192,128]{1,0:T(8,128)S(1)}, f32[192,128]{1,0:T(8,128)S(1)}, u32[]{:S(2)}, u32[]{:S(2)}) collective-permute-start(f32[192,128]{1,0:T(8,128)S(1)} %get-tuple-element.82), channel_id=1, source_target_pairs={{8,16},{16,8},{9,17},{17,9},{10,18},{18,10},{11,19},{19,11},{12,20... | collective-permute-start | bytes 294920 | tf_op jit(solution)/shard_map/ppermute | solution.py:853
  8.6 7.9 %collective-permute-start.4 = (f32[120,128]{1,0:T(8,128)S(1)}, f32[120,128]{1,0:T(8,128)S(1)}, u32[]{:S(2)}, u32[]{:S(2)}) collective-permute-start(f32[120,128]{1,0:T(8,128)S(1)} %get-tuple-element.84), channel_id=1, source_target_pairs={{0,8},{8,0},{16,24},{24,16},{1,9},{9,1},{17,25},{25,17},{2,10},{10... | collective-permute-start | bytes 184328 | tf_op jit(solution)/shard_map/ppermute | solution.py:853
  12.0 5.5 %collective-permute-start.5 = (f32[120,128]{1,0:T(8,128)S(1)}, f32[120,128]{1,0:T(8,128)S(1)}, u32[]{:S(2)}, u32[]{:S(2)}) collective-permute-start(f32[120,128]{1,0:T(8,128)S(1)} %get-tuple-element.85), channel_id=1, source_target_pairs={{8,16},{16,8},{9,17},{17,9},{10,18},{18,10},{11,19},{19,11},{12,20... | collective-permute-start | bytes 184328 | tf_op jit(solution)/shard_map/ppermute | solution.py:853
  18.4 5.8 %collective-permute-start.9 = (f32[216,128]{1,0:T(8,128)S(1)}, f32[216,128]{1,0:T(8,128)S(1)}, u32[]{:S(2)}, u32[]{:S(2)}) collective-permute-start(f32[216,128]{1,0:T(8,128)S(1)} %get-tuple-element.115), channel_id=1, source_target_pairs={{1,2},{2,1},{3,4},{4,3},{5,6},{6,5},{9,10},{10,9},{11,12},{12,11},... | collective-permute-start | bytes 331784 | tf_op jit(solution)/shard_map/ppermute | solution.py:853
  19.1 7.3 %collective-permute-start.8 = (f32[216,128]{1,0:T(8,128)S(1)}, f32[216,128]{1,0:T(8,128)S(1)}, u32[]{:S(2)}, u32[]{:S(2)}) collective-permute-start(f32[216,128]{1,0:T(8,128)S(1)} %get-tuple-element.114.m0), channel_id=1, source_target_pairs={{0,1},{1,0},{2,3},{3,2},{4,5},{5,4},{6,7},{7,6},{8,9},{9,8},{10,11... | collective-permute-start | bytes 331784 | tf_op jit(solution)/shard_map/ppermute | solution.py:853
  26.4 9.9 %collective-permute-start.10 = (f32[184,128]{1,0:T(8,128)S(1)}, f32[184,128]{1,0:T(8,128)S(1)}, u32[]{:S(2)}, u32[]{:S(2)}) collective-permute-start(f32[184,128]{1,0:T(8,128)S(1)} %get-tuple-element.116), channel_id=1, source_target_pairs={{0,8},{8,0},{16,24},{24,16},{1,9},{9,1},{17,25},{25,17},{2,10},{10... | collective-permute-start | bytes 282632 | tf_op jit(solution)/shard_map/ppermute | solution.py:853
  26.5 9.8 %collective-permute-start.11 = (f32[184,128]{1,0:T(8,128)S(1)}, f32[184,128]{1,0:T(8,128)S(1)}, u32[]{:S(2)}, u32[]{:S(2)}) collective-permute-start(f32[184,128]{1,0:T(8,128)S(1)} %get-tuple-element.117), channel_id=1, source_target_pairs={{8,16},{16,8},{9,17},{17,9},{10,18},{18,10},{11,19},{19,11},{12,20... | collective-permute-start | bytes 282632 | tf_op jit(solution)/shard_map/ppermute | solution.py:853
  30.7 2.5 %collective-permute-start.6 = (f32[112,128]{1,0:T(8,128)S(1)}, f32[112,128]{1,0:T(8,128)S(1)}, u32[]{:S(2)}, u32[]{:S(2)}) collective-permute-start(f32[112,128]{1,0:T(8,128)S(1)} %get-tuple-element.112), channel_id=1, source_target_pairs={{0,8},{8,0},{16,24},{24,16},{1,9},{9,1},{17,25},{25,17},{2,10},{10... | collective-permute-start | bytes 172040 | tf_op jit(solution)/shard_map/ppermute | solution.py:853
  30.8 5.5 %collective-permute-start.7 = (f32[112,128]{1,0:T(8,128)S(1)}, f32[112,128]{1,0:T(8,128)S(1)}, u32[]{:S(2)}, u32[]{:S(2)}) collective-permute-start(f32[112,128]{1,0:T(8,128)S(1)} %get-tuple-element.113), channel_id=1, source_target_pairs={{8,16},{16,8},{9,17},{17,9},{10,18},{18,10},{11,19},{19,11},{12,20... | collective-permute-start | bytes 172040 | tf_op jit(solution)/shard_map/ppermute | solution.py:853
